TPU v7x, 32 devices: a whole 2x2x4 slice. The times are simulated.
32 devices in a mesh: row: 16 (over z, x, core), col: 2 (over y).
Axes of the slice: x: 2, y: 2, z: 4, core: 2. Of those that a mesh axis runs over, the one named last changes fastest.
Arguments:
- node_feats: bfloat16 [49152, 512], P(('row', 'col')), may hold values from -6 to 6
- w_msg: bfloat16 [512, 512], replicated, may hold values from -0.25 to 0.25
- step_table: bfloat16 [1000, 512], replicated, may hold values from -3 to 3
- step_ids: int32 [49152], P(('row', 'col')), may hold values from 0 to 999
- tile_vals: bfloat16 [1152, 128, 128], P('row'), may hold values from -0.5 to 0.5
- tile_owner: int32 [1152, 1], P('row'), may hold values from 0 to 15; in each aligned block of 72 rows (0 to 71, 72 to 143, ...) at most 9 rows name the same one
- tile_dst_off: int32 [1152], P('row'), may hold values from 0 to 23
- tile_src: int32 [1152], P('row'), may hold values from 0 to 23
- cotangent: bfloat16 [512, 49152], P('col', 'row'), may hold values from -6 to 6
Outputs:
- aggregated: bfloat16 [512, 49152], P('col', 'row')
- feat_grad: bfloat16 [49152, 512], P(('row', 'col'))
- weight_grad: bfloat16 [512, 512], replicated
Inputs may be any that keep to these rules, and one draw needn't show every extreme that they name: `tile_owner`: among the 72 tiles of one index of row, at most 9 name the same owner row index, and some row index reaches 9.
All inputs are finite; a program needn't handle non-finite values.
Results may differ from a plain program's by a relative error of at most 0.012.
Values may be sent and summed in bfloat16 or wider, within the bound.
No kernel may reach another device: no remote copies, remote signals or barrier semaphores. Data moves between devices by JAX's collectives and lax.ppermute only.
A program may use at most 64 MiB of HBM per device.

v0:
```python
import functools

import jax
import jax.numpy as jnp
import numpy as np
from jax import lax
from jax.experimental import pallas as pl
from jax.experimental.pallas import tpu as pltpu
from jax.sharding import PartitionSpec as P


F32 = jnp.float32
BF16 = jnp.bfloat16
VMEM_LIMIT = 48 * 1024 * 1024
GRID_VMEM = 32 * 1024 * 1024
PARTS_VMEM = 20 * 1024 * 1024
SMALL_VMEM = 16 * 1024 * 1024


def gelu_value(v):
    return 0.5 * v * (1.0 + jax.scipy.special.erf(v / jnp.sqrt(2.0)))


def gelu_slope(v):
    return 0.5 * (1.0 + jax.scipy.special.erf(v / jnp.sqrt(2.0))) + v * jnp.exp(
        -0.5 * v * v
    ) / jnp.sqrt(2.0 * jnp.pi)


def ring_order(row_count):
    chips = row_count // 2
    bits = max(chips.bit_length() - 1, 0)
    nz = 1 << ((bits + 1) // 2)
    nx = chips // nz
    path = []
    for x in range(nx):
        zs = range(1, nz) if x % 2 == 0 else range(nz - 1, 0, -1)
        if nz == 1:
            zs = range(0)
        path += [(z, x) for z in zs]
    path += [(0, x) for x in range(nx - 1, -1, -1)]
    order = []
    for z, x in path:
        order += [(z * nx + x) * 2, (z * nx + x) * 2 + 1]
    return order


def add_tiles(acc_ref, row, owner, off, src, msg_ref, tiles_ref, side):
    per_part = msg_ref.shape[2] // side

    def step(t, carry):
        @pl.when(owner[t] == row)
        def _():
            s = src[t]
            col = pl.multiple_of(lax.rem(s, per_part) * side, side)
            feats = msg_ref[lax.div(s, per_part), :, pl.ds(col, side)]
            part = lax.dot_general(
                feats, tiles_ref[t], (((1,), (1,)), ((), ())), preferred_element_type=F32
            )
            at = pl.ds(pl.multiple_of(off[t] * side, side), side)
            acc_ref[:, at] = acc_ref[:, at] + part

        return carry

    lax.fori_loop(0, tiles_ref.shape[0], step, 0)


def hop_kernel(which, has_recv, side, rows, owner, off, src, *refs):
    if has_recv:
        recv_ref, msg_ref, tiles_ref, _, out_ref, acc_ref = refs
        acc_ref[...] = recv_ref[...].astype(F32)
    else:
        msg_ref, tiles_ref, _, out_ref, acc_ref = refs
        acc_ref[...] = jnp.zeros_like(acc_ref)
    add_tiles(acc_ref, rows[which], owner, off, src, msg_ref, tiles_ref, side)
    out_ref[...] = acc_ref[...].astype(out_ref.dtype)


def hop(which, half, recv, rows, owner, off, src, msg, tiles, gate, width):
    parts, feats, part_nodes = msg.shape
    fh = feats // 2
    side = tiles.shape[1]
    args = ([recv] if recv is not None else []) + [msg, tiles, gate]
    vm = pl.BlockSpec(memory_space=pltpu.VMEM)
    full = pl.BlockSpec((fh, width), lambda i, *_: (0, 0))
    specs = ([full] if recv is not None else []) + [
        pl.BlockSpec((parts, fh, part_nodes), lambda i, *_: (0, half, 0)),
        pl.BlockSpec(tiles.shape, lambda i, *_: (0, 0, 0)),
        pl.BlockSpec(memory_space=pl.ANY),
    ]
    return pl.pallas_call(
        functools.partial(hop_kernel, which, recv is not None, side),
        out_shape=jax.ShapeDtypeStruct((fh, width), BF16),
        grid_spec=pltpu.PrefetchScalarGridSpec(
            num_scalar_prefetch=4,
            grid=(1,),
            in_specs=specs,
            out_specs=full,
            scratch_shapes=[pltpu.VMEM((fh, width), F32)],
        ),
        compiler_params=pltpu.CompilerParams(vmem_limit_bytes=VMEM_LIMIT),
        cost_estimate=pl.CostEstimate(
            flops=2 * fh * side * side * 9, bytes_accessed=6 * 2**20, transcendentals=0
        ),
        name="hop",
    )(rows, owner, off, src, *args)


def last_kernel(which, side, rows, owner, off, src, p0, m0, p1, m1, msg_ref, tiles_ref, out_ref, acc_ref):
    fh = p0.shape[0]
    acc_ref[:fh, :] = p0[...].astype(F32) + m0[...].astype(F32)
    acc_ref[fh:, :] = p1[...].astype(F32) + m1[...].astype(F32)
    add_tiles(acc_ref, rows[which], owner, off, src, msg_ref, tiles_ref, side)
    out_ref[...] = acc_ref[...].astype(out_ref.dtype)


def last_hop(which, recvs, rows, owner, off, src, msg, tiles, width):
    _, feats, _ = msg.shape
    side = tiles.shape[1]
    half = pl.BlockSpec((feats // 2, width), lambda i, *_: (0, 0))
    return pl.pallas_call(
        functools.partial(last_kernel, which, side),
        out_shape=jax.ShapeDtypeStruct((feats, width), BF16),
        grid_spec=pltpu.PrefetchScalarGridSpec(
            num_scalar_prefetch=4,
            grid=(1,),
            in_specs=[half] * 4
            + [
                pl.BlockSpec(msg.shape, lambda i, *_: (0, 0, 0)),
                pl.BlockSpec(tiles.shape, lambda i, *_: (0, 0, 0)),
            ],
            out_specs=pl.BlockSpec((feats, width), lambda i, *_: (0, 0)),
            scratch_shapes=[pltpu.VMEM((feats, width), F32)],
        ),
        compiler_params=pltpu.CompilerParams(vmem_limit_bytes=VMEM_LIMIT),
        name="last_hop",
    )(rows, owner, off, src, *recvs, msg, tiles)


def back_kernel(side, owner, off, src, grads_ref, tiles_ref, *refs):
    out_ref, buf_ref, acc_ref, sem = refs[-4:]
    count = tiles_ref.shape[0]
    per_part = out_ref.shape[2] // side

    def fetch(t):
        at = pl.ds(pl.multiple_of(off[t] * side, side), side)
        return pltpu.make_async_copy(grads_ref.at[owner[t], :, at], buf_ref.at[t], sem.at[t])

    def begin(t, carry):
        fetch(t).start()
        return carry

    lax.fori_loop(0, count, begin, 0)
    acc_ref[...] = jnp.zeros_like(acc_ref)

    def step(t, carry):
        fetch(t).wait()
        term = jnp.dot(buf_ref[t], tiles_ref[t], preferred_element_type=F32)
        s = src[t]
        at = pl.ds(pl.multiple_of(lax.rem(s, per_part) * side, side), side)
        part = lax.div(s, per_part)
        acc_ref[part, :, at] = acc_ref[part, :, at] + term
        return carry

    lax.fori_loop(0, count, step, 0)
    out_ref[...] = acc_ref[...].astype(out_ref.dtype)


def back(owner, off, src, grads, tiles, parts, after):
    _, feats, width = grads.shape
    count, side, _ = tiles.shape
    shape = (parts, feats, width // parts)
    return pl.pallas_call(
        functools.partial(back_kernel, side),
        out_shape=jax.ShapeDtypeStruct(shape, BF16),
        grid_spec=pltpu.PrefetchScalarGridSpec(
            num_scalar_prefetch=3,
            grid=(1,),
            in_specs=[
                pl.BlockSpec(memory_space=pl.ANY),
                pl.BlockSpec(tiles.shape, lambda i, *_: (0, 0, 0)),
            ]
            + [pl.BlockSpec(memory_space=pl.ANY)] * len(after),
            out_specs=pl.BlockSpec(shape, lambda i, *_: (0, 0, 0)),
            scratch_shapes=[
                pltpu.VMEM((count, feats, side), BF16),
                pltpu.VMEM(shape, F32),
                pltpu.SemaphoreType.DMA((count,)),
            ],
        ),
        compiler_params=pltpu.CompilerParams(vmem_limit_bytes=VMEM_LIMIT),
        cost_estimate=pl.CostEstimate(
            flops=2 * feats * side * side * count, bytes_accessed=30 * 2**20, transcendentals=0
        ),
        name="back",
    )(owner, off, src, grads, tiles, *after)


def ring_device(
    node_feats,
    w_msg,
    step_table,
    step_ids,
    tile_vals,
    tile_owner,
    tile_dst_off,
    tile_src,
    cotangent,
):
    row_count = lax.axis_size("row")
    col_count = lax.axis_size("col")
    feats, width = cotangent.shape
    owner = tile_owner[:, 0]

    ring = ring_order(row_count)
    pos_of = np.argsort(np.array(ring))
    up = [(ring[p], ring[(p + 1) % row_count]) for p in range(row_count)]
    down = [(b, a) for a, b in up]
    far, near = row_count // 2, row_count - 1 - row_count // 2
    chains = [
        (0, 1, far),
        (0, -1, near),
        (1, 1, near),
        (1, -1, far),
    ]
    table = []
    for half, sign, hops in chains:
        for s in range(hops):
            table.append([ring[(pos_of[r] + sign * (hops - s)) % row_count] for r in range(row_count)])
    table.append(list(range(row_count)))
    table = jnp.asarray(np.array(table, dtype=np.int32).T)
    rows = lax.dynamic_index_in_dim(table, lax.axis_index("row"), 0, keepdims=False)

    grads = lax.all_gather(cotangent, "row", axis=0)

    step_hot = (
        step_ids[:, None] == jnp.arange(step_table.shape[0], dtype=jnp.int32)[None, :]
    ).astype(BF16)
    dims = (((0,), (1,)), ((), ()))
    pre_t = lax.dot_general(w_msg, node_feats, dims, preferred_element_type=F32)
    pre_t = pre_t + lax.dot_general(step_table, step_hot, dims, preferred_element_type=F32)
    msg_t = gelu_value(pre_t).astype(BF16)
    pre_t = lax.optimization_barrier(pre_t)
    nodes = msg_t.shape[1]
    msg = lax.all_to_all(
        msg_t.reshape(col_count, feats, nodes), "col", split_axis=0, concat_axis=0, tiled=True
    )

    held = [None] * len(chains)
    begun = []
    first = [sum(c[2] for c in chains[:i]) for i in range(len(chains))]
    for s in range(far):
        for i, (half, sign, hops) in enumerate(chains):
            skip = far - hops
            if s < skip:
                continue
            k = s - skip
            out = hop(
                first[i] + k, half, held[i], rows, owner, tile_dst_off, tile_src, msg, tile_vals, grads, width
            )
            if s == 0:
                begun.append(out)
            held[i] = lax.ppermute(out, "row", up if sign > 0 else down)
    which = sum(c[2] for c in chains)
    aggregated = last_hop(
        which, held, rows, owner, tile_dst_off, tile_src, msg, tile_vals, width
    )

    dmsg = back(owner, tile_dst_off, tile_src, grads, tile_vals, col_count, begun)
    return finish(node_feats, w_msg, pre_t, dmsg, aggregated)


GROUP = 4


def each_tile(meta, base, chip, product, add):
    low, high = meta[base + chip], meta[base + chip + 1]

    def step(g, carry):
        at = [low + g * GROUP + u for u in range(GROUP)]
        use = [jnp.minimum(i, high - 1) for i in at]
        parts = [product(i) for i in use]
        for i, j, part in zip(at, use, parts):
            add(j, jnp.where(i < high, part, 0.0))
        return carry

    lax.fori_loop(0, lax.div(high - low + GROUP - 1, GROUP), step, 0)


def parts_kernel(meta_own, meta_other, msg_own, msg_other, tiles_own, tiles_other, out_ref):
    count, side, _ = tiles_own.shape
    per_part = msg_own.shape[2] // side
    for q, (meta, msg, tiles) in enumerate(
        ((meta_own, msg_own, tiles_own), (meta_other, msg_other, tiles_other))
    ):

        def product(i, meta=meta, msg=msg, tiles=tiles):
            s = meta[2 * count + i]
            at = pl.ds(pl.multiple_of(lax.rem(s, per_part) * side, side), side)
            return lax.dot_general(
                msg[lax.div(s, per_part), :, at],
                tiles[meta[3 * count + i]],
                (((1,), (1,)), ((), ())),
                preferred_element_type=F32,
            )

        def step(g, carry, q=q, product=product):
            at = [g * GROUP + u for u in range(GROUP)]
            for i, part in zip(at, [product(i) for i in at]):
                out_ref[q, i] = part.astype(BF16)
            return carry

        lax.fori_loop(0, count // GROUP, step, 0)


SMEM = pl.BlockSpec(memory_space=pltpu.SMEM)
VMEM = pl.BlockSpec(memory_space=pltpu.VMEM)


def tile_parts(meta_own, meta_other, msg_own, msg_other, tiles_own, tiles_other):
    count, side, _ = tiles_own.shape
    feats = msg_own.shape[1]
    return pl.pallas_call(
        parts_kernel,
        out_shape=jax.ShapeDtypeStruct((2, count, feats, side), BF16),
        in_specs=[SMEM] * 2 + [VMEM] * 4,
        out_specs=VMEM,
        compiler_params=pltpu.CompilerParams(vmem_limit_bytes=PARTS_VMEM),
        cost_estimate=pl.CostEstimate(flops=2**30, bytes_accessed=12 * 2**20, transcendentals=0),
        name="tile_parts",
    )(meta_own, meta_other, msg_own, msg_other, tiles_own, tiles_other)


def sum_kernel(spec, ids, meta_own, meta_other, parts, *refs):
    chips, picks, low, split = spec
    recvs, rest = refs[: len(picks)], refs[len(picks) :]
    acc = rest[-1]
    outs = rest[:-1] if split else rest
    _, count, _, side = parts.shape
    feats = acc.shape[-2]
    base = 4 * count
    total = None
    for ref, pick in zip(recvs, picks):
        part = ref[...] if pick is None else ref[pick]
        part = part.reshape(acc.shape)
        if len(picks) > 1:
            part = part.astype(F32)
        total = part if total is None else total + part
    acc[...] = jnp.zeros_like(acc) if total is None else total.astype(acc.dtype)
    core = ids[ids.shape[0] - 1]
    for m, which in enumerate(chips):
        chip = ids[which]
        for q, meta in enumerate((meta_own, meta_other)):

            def step(i, carry, m=m, q=q, meta=meta):
                a = jnp.bitwise_xor(jnp.bitwise_and(meta[i], 1), core)
                at = (m, a) if len(chips) > 1 else (a,)
                to = pl.ds(pl.multiple_of(meta[count + i] * side, side), side)
                at = at + (slice(None), to)
                part = parts[q, i, low : low + feats, :].astype(F32)
                acc[at] = (acc[at].astype(F32) + part).astype(acc.dtype)
                return carry

            lax.fori_loop(meta[base + chip], meta[base + chip + 1], step, 0)
    if split:
        for a in (0, 1):
            outs[a][...] = acc[a].astype(BF16)


def tile_sums(env, chips, recvs, low, feats, width, split=False):
    ids, meta_own, meta_other, parts, _, _ = env
    shape = (2, feats, width) if len(chips) == 1 else (len(chips), 2, feats, width)
    if split:
        out = [jax.ShapeDtypeStruct((feats, width), BF16)] * 2
    else:
        out = jax.ShapeDtypeStruct(shape, BF16)
    spec = (tuple(chips), tuple(p for _, p in recvs), low, split)
    return pl.pallas_call(
        functools.partial(sum_kernel, spec),
        out_shape=out,
        in_specs=[SMEM] * 3 + [VMEM] * (1 + len(recvs)),
        out_specs=[VMEM] * 2 if split else VMEM,
        scratch_shapes=[pltpu.VMEM(shape, F32)] if split else [],
        compiler_params=pltpu.CompilerParams(vmem_limit_bytes=SMALL_VMEM),
        cost_estimate=pl.CostEstimate(flops=2**20, bytes_accessed=3 * 2**20, transcendentals=0),
        name="tile_sums",
    )(ids, meta_own, meta_other, parts, *[a for a, _ in recvs])


def grad_kernel(spec, ids, meta_own, meta_other, tiles_own, tiles_other, *refs):
    chips, has_sum, final = spec
    arrays, rest = refs[: len(chips)], refs[len(chips) :]
    count, side, _ = tiles_own.shape
    base = 4 * count
    if final:
        outs, acc = rest[-3:-1], rest[-1]
    else:
        acc = rest[-1]
    acc[...] = rest[0][...] if has_sum else jnp.zeros_like(acc)
    per_part = acc.shape[3] // side
    core = ids[ids.shape[0] - 1]
    for which, array in zip(chips, arrays):
        chip = ids[which]
        for q, (meta, tiles) in enumerate(((meta_own, tiles_own), (meta_other, tiles_other))):

            def product(i, meta=meta, tiles=tiles, array=array):
                a = jnp.bitwise_xor(jnp.bitwise_and(meta[i], 1), core)
                at = pl.ds(pl.multiple_of(meta[count + i] * side, side), side)
                return jnp.dot(
                    array[a, :, at], tiles[meta[3 * count + i]], preferred_element_type=F32
                )

            def add(i, term, q=q, meta=meta):
                s = meta[2 * count + i]
                part = lax.div(s, per_part)
                to = pl.ds(pl.multiple_of(lax.rem(s, per_part) * side, side), side)
                acc[q, part, :, to] = acc[q, part, :, to] + term

            each_tile(meta, base, chip, product, add)
    if final:
        for q in (0, 1):
            outs[q][...] = acc[q].astype(BF16)


def grad_sums(env, chips, arrays, so_far, parts, final):
    ids, meta_own, meta_other, _, tiles_own, tiles_other = env
    smem = pl.BlockSpec(memory_space=pltpu.SMEM)
    vmem = pl.BlockSpec(memory_space=pltpu.VMEM)
    _, feats, width = arrays[0].shape
    shape = (2, parts, feats, width // parts)
    if final:
        out = [jax.ShapeDtypeStruct(shape[1:], BF16)] * 2
        scratch = [pltpu.VMEM(shape, F32)]
    else:
        out = jax.ShapeDtypeStruct(shape, F32)
        scratch = []
    sums = [] if so_far is None else [so_far]
    return pl.pallas_call(
        functools.partial(grad_kernel, (tuple(chips), bool(sums), final)),
        out_shape=out,
        in_specs=[smem] * 3 + [vmem] * (2 + len(arrays) + len(sums)),
        out_specs=[vmem] * 2 if final else vmem,
        scratch_shapes=scratch,
        compiler_params=pltpu.CompilerParams(vmem_limit_bytes=GRID_VMEM),
        cost_estimate=pl.CostEstimate(flops=2**28, bytes_accessed=8 * 2**20, transcendentals=0),
        name="grad_sums",
    )(ids, meta_own, meta_other, tiles_own, tiles_other, *arrays, *sums)


def sorted_meta(owner, off, src, chips):
    count = owner.shape[0]
    key = owner // 2
    place = jnp.arange(count, dtype=jnp.int32)
    before = (key[None, :] < key[:, None]) | (
        (key[None, :] == key[:, None]) & (place[None, :] < place[:, None])
    )
    pos = jnp.sum(before.astype(jnp.int32), axis=1)
    hot = (pos[:, None] == place[None, :]).astype(jnp.int32)
    values = jnp.stack([owner, off, src, place])
    ordered = jnp.sum(values[:, :, None] * hot[None], axis=1)
    bounds = jnp.arange(chips + 2, dtype=jnp.int32)
    starts = jnp.sum((key[:, None] < bounds[None, :]).astype(jnp.int32), axis=0)
    return jnp.concatenate([ordered.reshape(-1), starts])


def grid_device(
    node_feats,
    w_msg,
    step_table,
    step_ids,
    tile_vals,
    tile_owner,
    tile_dst_off,
    tile_src,
    cotangent,
):
    row_count = lax.axis_size("row")
    col_count = lax.axis_size("col")
    feats, width = cotangent.shape
    slab = feats // 2
    feats_a = max(16, (3 * slab // 8) // 16 * 16)
    feats_b = slab - feats_a
    nz = row_count // 4
    chips = row_count // 2
    me = lax.axis_index("row")
    core = jnp.bitwise_and(me, 1)
    every = range(row_count)
    swap = [(r, r ^ 1) for r in every]

    def z_move(sign, ok):
        return [(r, r + 4 * sign) for r in every if 0 <= r // 4 + sign < nz and ok(r // 4)]

    def x_move(ok):
        return [(r, r ^ 2) for r in every if ok(r // 4)]

    def rel(dz, dx):
        return (dz + nz - 1) * 2 + dx

    def turn(j, dx):
        return (2 * nz - 1) * 2 + j * 2 + dx

    table = np.zeros((row_count, (2 * nz - 1) * 2 + 2 * nz + 1), np.int32)
    for r in every:
        z, x, c = r // 4, (r // 2) % 2, r % 2
        for dx in (0, 1):
            for dz in range(1 - nz, nz):
                inside = 0 <= z + dz < nz
                table[r, rel(dz, dx)] = (z + dz) * 2 + (x ^ dx) if inside else chips
            for j in range(nz):
                table[r, turn(j, dx)] = ((z + j) % nz) * 2 + (x ^ dx)
        table[r, -1] = c
    ids = lax.dynamic_index_in_dim(jnp.asarray(table), me, 0, keepdims=False)

    def permute(a, pairs):
        return lax.ppermute(a, "row", pairs)

    def mine_and_other(a, axis):
        size = a.shape[axis] // 2
        mine = lax.dynamic_slice_in_dim(a, core * size, size, axis)
        other = lax.dynamic_slice_in_dim(a, (1 - core) * size, size, axis)
        return mine, other

    def in_order(mine, other, axis):
        first = jnp.where(core == 0, mine, other)
        second = jnp.where(core == 0, other, mine)
        return jnp.concatenate([first, second], axis=axis)

    mine, other = mine_and_other(cotangent, 0)
    shard = jnp.stack([mine, permute(other, swap)])
    line = {0: shard}
    across = {0: permute(shard, x_move(lambda z: True))}
    for k in range(1, nz):
        for sign in (-1, 1):
            pairs = z_move(-sign, lambda z: 0 <= z + sign * (k - 1) < nz)
            line[sign * k] = permute(line[sign * (k - 1)], pairs)
        for sign in (-1, 1):
            pairs = x_move(lambda z: 0 <= z + sign * k < nz)
            across[sign * k] = permute(line[sign * k], pairs)

    meta_own = sorted_meta(tile_owner[:, 0], tile_dst_off, tile_src, chips)
    meta_other = permute(meta_own, swap)
    tiles_other = permute(tile_vals, swap)

    step_hot = (
        step_ids[:, None] == jnp.arange(step_table.shape[0], dtype=jnp.int32)[None, :]
    ).astype(BF16)
    dims = (((0,), (1,)), ((), ()))
    pre_t = lax.dot_general(w_msg, node_feats, dims, preferred_element_type=F32)
    pre_t = pre_t + lax.dot_general(step_table, step_hot, dims, preferred_element_type=F32)
    msg_t = gelu_value(pre_t).astype(BF16)
    pre_t = lax.optimization_barrier(pre_t)
    nodes = msg_t.shape[1]
    msg = lax.all_to_all(
        msg_t.reshape(col_count, feats, nodes), "col", split_axis=0, concat_axis=0, tiled=True
    )
    msg_own, other = mine_and_other(msg, 1)
    msg_other = permute(other, swap)
    parts = tile_parts(meta_own, meta_other, msg_own, msg_other, tile_vals, tiles_other)
    env = (ids, meta_own, meta_other, parts, tile_vals, tiles_other)

    def sums_a(chip, recvs, split=False):
        return tile_sums(env, [chip], recvs, 0, feats_a, width, split=split)

    def sums_b(picks, recvs, split=False):
        return tile_sums(env, picks, recvs, feats_a, feats_b, width, split=split)

    def known(a):
        return [] if a is None else [(a, None)]

    from_x = {j: permute(sums_a(turn(j, 1), []), x_move(lambda z: True)) for j in range(nz)}
    flow_a, flow_b = {-1: None, 1: None}, {-1: None, 1: None}
    for d in range(nz - 1, 0, -1):
        for sign in (1, -1):
            pairs = z_move(sign, lambda z: 0 <= z + sign * d < nz)
            out = sums_b([rel(sign * d, 0), rel(sign * d, 1)], known(flow_b[sign]))
            flow_b[sign] = permute(out, pairs)
            out = sums_a(rel(sign * d, 0), known(from_x[sign * d % nz]) + known(flow_a[sign]))
            flow_a[sign] = permute(out, pairs)
    recv_b = permute(sums_b([rel(0, 1)], [(flow_b[1], 1), (flow_b[-1], 1)]), x_move(lambda z: True))
    keep_b, send_b = sums_b(
        [rel(0, 0)], [(flow_b[1], 0), (flow_b[-1], 0), (recv_b, None)], split=True
    )
    keep_a, send_a = sums_a(
        rel(0, 0), known(from_x[0]) + known(flow_a[1]) + known(flow_a[-1]), split=True
    )
    other_a, other_b = permute(send_a, swap), permute(send_b, swap)
    aggregated = in_order(
        jnp.concatenate([keep_a, keep_b]), jnp.concatenate([other_a, other_b]), 0
    )

    def grads(dx, steps, so_far, final=False):
        arrays = [(line, across)[dx][dz] for dz in steps]
        return grad_sums(env, [rel(dz, dx) for dz in steps], arrays, so_far, col_count, final)

    near = [dz for dz in line if abs(dz) <= 1]
    far = [dz for dz in line if abs(dz) > 1]
    acc = grads(0, near, None)
    acc = grads(0, far, acc)
    acc = grads(1, near, acc)
    own, send = grads(1, far, acc, True)
    dmsg = in_order(own, permute(send, swap), 1)
    return finish(node_feats, w_msg, pre_t, dmsg, aggregated)


def finish(node_feats, w_msg, pre_t, dmsg, aggregated):
    dims = (((0,), (1,)), ((), ()))
    dmsg_rows = lax.all_to_all(dmsg, "col", split_axis=0, concat_axis=0, tiled=True)
    dmsg_rows = dmsg_rows.reshape(pre_t.shape)
    dpre_t = (dmsg_rows.astype(F32) * gelu_slope(pre_t)).astype(BF16)
    feat_grad = lax.dot_general(dpre_t, w_msg, dims, preferred_element_type=F32).astype(BF16)
    weight_term = lax.dot_general(
        node_feats, dpre_t, dims, preferred_element_type=F32
    ).astype(BF16)
    devices = lax.axis_size("row") * lax.axis_size("col")
    hidden = weight_term.shape[0]
    rows_each = hidden // devices
    axes = ("row", "col")
    shares = lax.all_to_all(
        weight_term.reshape(devices, rows_each, hidden), axes, split_axis=0, concat_axis=0, tiled=True
    )
    share = jnp.sum(shares.astype(F32), axis=0).astype(BF16)
    weight_grad = lax.all_to_all(
        jnp.broadcast_to(share[None], (devices,) + share.shape), axes, split_axis=0, concat_axis=0, tiled=True
    ).reshape(hidden, hidden)
    return (aggregated, feat_grad, weight_grad)


def solution(mesh):
    rows = mesh.shape["row"]
    in_grid = rows == 16

    def per_device(*args):
        return (grid_device if in_grid else ring_device)(*args)

    return jax.shard_map(
        per_device,
        mesh=mesh,
        in_specs=(
            P(("row", "col"), None),
            P(),
            P(),
            P(("row", "col")),
            P("row", None, None),
            P("row", None),
            P("row"),
            P("row"),
            P("col", "row"),
        ),
        out_specs=(P("col", "row"), P(("row", "col"), None), P()),
        check_vma=False,
    )
```

profile of v0, /device:TPU:0, one launch (start us, length us, event | category | flops | bytes accessed | tf_op | source)
XLA Modules:
  0.0 372.4 jit_solution(675338837001574894)
XLA Ops:
  0.7 2.5 dynamic-slice_bitcast_fusion
  3.7 2.1 fusion.1
  5.8 2.9 multiply_convert_fusion
  8.7 4.7 %all-to-all-start = ((bf16[2,256,1536]{2,1,0:T(8,128)(2,1)}), bf16[2,256,1536]{2,1,0:T(8,128)(2,1)}, u32[]{:S(2)}, u32[]{:S(2)}) async-start(bf16[2,256,1536]{2,1,0:T(8,128)(2,1)} %bitcast.7), calls=%async_computation | async-start | bytes 3145728 | tf_op jit(solution)/shard_map/all_to_all | solution.py:553
  14.4 1.5 pad_maximum_fusion.1.refs_0_
  16.0 6.1 %collective-permute-start.23 = (bf16[2,128,3072]{2,1,0:T(8,128)(2,1)S(1)}, bf16[2,128,3072]{2,1,0:T(8,128)(2,1)}, u32[]{:S(2)}, u32[]{:S(2)}) collective-permute-start(bf16[2,128,3072]{2,1,0:T(8,128)(2,1)S(1)} %pad_maximum_fusion.1.refs_0_), channel_id=1, source_target_pairs={{0,8},{2,10},{4,12},{6,14},{8,16},{10,18},{12,20},{14,22},{16,24},... | collective-permute-start | bytes 4718600 | tf_op jit(solution)/shard_map/ppermute | solution.py:515
  24.1 1.6 collective-permute-start.33
  25.7 8.8 %all-to-all-done = bf16[2,256,1536]{2,1,0:T(8,128)(2,1)} async-done(((bf16[2,256,1536]{2,1,0:T(8,128)(2,1)}), bf16[2,256,1536]{2,1,0:T(8,128)(2,1)}, u32[]{:S(2)}, u32[]{:S(2)}) %all-to-all-start) | async-done | bytes 1572896 | tf_op jit(solution)/shard_map/all_to_all | solution.py:553
  34.5 2.4 constant_dynamic-slice_fusion.1
  36.8 17.9 %collective-permute-done.23.refs_1_ = bf16[2,128,3072]{2,1,0:T(8,128)(2,1)} collective-permute-done((bf16[2,128,3072]{2,1,0:T(8,128)(2,1)S(1)}, bf16[2,128,3072]{2,1,0:T(8,128)(2,1)}, u32[]{:S(2)}, u32[]{:S(2)}) %collective-permute-start.23) | collective-permute-done | bytes 1572896 | tf_op jit(solution)/shard_map/ppermute | solution.py:515
  54.7 1.8 collective-permute-start.24
  56.5 3.6 collective-permute-done.26.refs_2_
  62.3 1.8 collective-permute-start.34
  64.1 3.4 collective-permute-start.35
  70.5 10.0 %tile_parts.1.parts = bf16[2,72,128,128]{3,2,1,0:T(8,128)(2,1)S(1)} custom-call(s32[298]{0:T(512)S(1)} %pad_add_fusion.1.meta_own, s32[298]{0:T(512)S(1)} %collective-permute-done.meta_other, bf16[2,128,1536]{2,1,0:T(8,128)(2,1)S(1)} %copy-done.5, bf16[2,128,1536]{2,1,0:T(8,128)(2,1)S(1)} %copy-done.21, bf16[72,128,128]{2,1,0:T(8,128)(2,1)} %tiles_own.9, ...), custom_call_target="tpu_custom_call" | custom-call | flops 1073741824 | bytes 12582912 | tf_op jit(solution)/shard_map/tile_parts/pallas_call | solution.py:323
  83.1 13.0 %collective-permute-start.13 = (bf16[2,2,80,3072]{3,2,1,0:T(8,128)(2,1)S(1)}, bf16[2,2,80,3072]{3,2,1,0:T(8,128)(2,1)S(1)}, u32[]{:S(2)}, u32[]{:S(2)}) collective-permute-start(bf16[2,2,80,3072]{3,2,1,0:T(8,128)(2,1)S(1)} %tile_sums.30), channel_id=1, source_target_pairs={{0,8},{2,10},{4,12},{6,14},{1,9},{3,11},{5,13},{7,15}} | collective-permute-start | bytes 5898248 | tf_op jit(solution)/shard_map/ppermute | solution.py:515
  96.1 1.5 collective-permute-done.27.refs_1_
  99.7 1.8 collective-permute-done.35.refs_2_
  102.3 3.4 collective-permute-start.28
  107.2 29.3 %collective-permute-done.13.refs_0_ = bf16[2,2,80,3072]{3,2,1,0:T(8,128)(2,1)S(1)} collective-permute-done((bf16[2,2,80,3072]{3,2,1,0:T(8,128)(2,1)S(1)}, bf16[2,2,80,3072]{3,2,1,0:T(8,128)(2,1)S(1)}, u32[]{:S(2)}, u32[]{:S(2)}) %collective-permute-start.13) | collective-permute-done | bytes 1966112 | tf_op jit(solution)/shard_map/ppermute | solution.py:515
  137.3 3.4 collective-permute-start.32
  140.7 2.8 tile_sums.31
  143.5 5.7 %collective-permute-start.14 = (bf16[2,2,80,3072]{3,2,1,0:T(8,128)(2,1)}, bf16[2,2,80,3072]{3,2,1,0:T(8,128)(2,1)}, u32[]{:S(2)}, u32[]{:S(2)}) collective-permute-start(bf16[2,2,80,3072]{3,2,1,0:T(8,128)(2,1)} %tile_sums.31), channel_id=1, source_target_pairs={{0,8},{2,10},{4,12},{6,14},{8,16},{10,18},{12,20},{14,22},{1,9},{3... | collective-permute-start | bytes 5898248 | tf_op jit(solution)/shard_map/ppermute | solution.py:515
  149.2 1.6 tile_sums.20
  151.5 1.6 tile_sums.22
  155.7 1.8 tile_sums.21
  157.5 18.9 %collective-permute-done.32.refs_3_ = bf16[2,128,3072]{2,1,0:T(8,128)(2,1)S(1)} collective-permute-done((bf16[2,128,3072]{2,1,0:T(8,128)(2,1)S(1)}, bf16[2,128,3072]{2,1,0:T(8,128)(2,1)S(1)}, u32[]{:S(2)}, u32[]{:S(2)}) %collective-permute-start.32) | collective-permute-done | bytes 1572896 | tf_op jit(solution)/shard_map/ppermute | solution.py:515
  177.6 1.5 collective-permute-start.5
  179.1 5.4 %grad_sums.4.refs_4_ = f32[2,2,128,1536]{3,2,1,0:T(8,128)S(1)} custom-call(s32[23]{0:T(128)S(1)} %fusion.12.ids, s32[298]{0:T(512)S(1)} %pad_add_fusion.1.meta_own, s32[298]{0:T(512)S(1)} %collective-permute-done.meta_other, bf16[72,128,128]{2,1,0:T(8,128)(2,1)} %tiles_own.9, bf16[72,128,128]{2,1,0:T(8,128)(2,1)} %collective-permute-done.2.tiles_other, ...), custom_call_target="tpu_custom_call" | custom-call | flops 268435456 | bytes 8388608 | tf_op jit(solution)/shard_map/grad_sums/pallas_call | solution.py:438
  184.5 5.8 %grad_sums.5.refs_3_ = f32[2,2,128,1536]{3,2,1,0:T(8,128)S(1)} custom-call(s32[23]{0:T(128)S(1)} %fusion.12.ids, s32[298]{0:T(512)S(1)} %pad_add_fusion.1.meta_own, s32[298]{0:T(512)S(1)} %collective-permute-done.meta_other, bf16[72,128,128]{2,1,0:T(8,128)(2,1)} %tiles_own.9, bf16[72,128,128]{2,1,0:T(8,128)(2,1)} %collective-permute-done.2.tiles_other, ...), custom_call_target="tpu_custom_call" | custom-call | flops 268435456 | bytes 8388608 | tf_op jit(solution)/shard_map/grad_sums/pallas_call | solution.py:438
  190.3 6.3 %grad_sums.6.refs_4_ = f32[2,2,128,1536]{3,2,1,0:T(8,128)S(1)} custom-call(s32[23]{0:T(128)S(1)} %fusion.12.ids, s32[298]{0:T(512)S(1)} %pad_add_fusion.1.meta_own, s32[298]{0:T(512)S(1)} %collective-permute-done.meta_other, bf16[72,128,128]{2,1,0:T(8,128)(2,1)} %tiles_own.9, bf16[72,128,128]{2,1,0:T(8,128)(2,1)} %collective-permute-done.2.tiles_other, ...), custom_call_target="tpu_custom_call" | custom-call | flops 268435456 | bytes 8388608 | tf_op jit(solution)/shard_map/grad_sums/pallas_call | solution.py:438
  199.5 5.9 %grad_sums.7 = (bf16[2,128,1536]{2,1,0:T(8,128)(2,1)S(1)}, bf16[2,128,1536]{2,1,0:T(8,128)(2,1)}) custom-call(s32[23]{0:T(128)S(1)} %fusion.12.ids, s32[298]{0:T(512)S(1)} %pad_add_fusion.1.meta_own, s32[298]{0:T(512)S(1)} %collective-permute-done.meta_other, bf16[72,128,128]{2,1,0:T(8,128)(2,1)} %tiles_own.9, ...), custom_call_target="tpu_custom_call" | custom-call | flops 268435456 | bytes 8388608 | tf_op jit(solution)/shard_map/grad_sums/pallas_call | solution.py:438
  205.5 1.4 tile_sums.26
  206.9 1.5 collective-permute-start.10
  208.4 1.6 tile_sums.23
  210.0 12.0 %collective-permute-start.7 = (bf16[2,48,3072]{2,1,0:T(8,128)(2,1)}, bf16[2,48,3072]{2,1,0:T(8,128)(2,1)}, u32[]{:S(2)}, u32[]{:S(2)}) collective-permute-start(bf16[2,48,3072]{2,1,0:T(8,128)(2,1)} %tile_sums.23), channel_id=1, source_target_pairs={{0,8},{2,10},{4,12},{6,14},{1,9},{3,11},{5,13},{7,15}} | collective-permute-start | bytes 1769480 | tf_op jit(solution)/shard_map/ppermute | solution.py:515
  222.0 2.0 tile_sums.35
  225.3 3.4 tile_sums.32
  229.6 6.3 %collective-permute-start.15 = (bf16[2,2,80,3072]{3,2,1,0:T(8,128)(2,1)}, bf16[2,2,80,3072]{3,2,1,0:T(8,128)(2,1)}, u32[]{:S(2)}, u32[]{:S(2)}) collective-permute-start(bf16[2,2,80,3072]{3,2,1,0:T(8,128)(2,1)} %tile_sums.32), channel_id=1, source_target_pairs={{0,8},{2,10},{4,12},{6,14},{8,16},{10,18},{12,20},{14,22},{16,24},... | collective-permute-start | bytes 5898248 | tf_op jit(solution)/shard_map/ppermute | solution.py:515
  235.9 2.3 copy-done.2
  239.3 2.1 tile_sums.27
  241.3 1.6 collective-permute-start.11
  243.0 2.5 tile_sums.24
  245.4 2.1 collective-permute-start.8
  250.1 4.6 %all-to-all-start.1 = ((bf16[2,256,1536]{2,1,0:T(8,128)(2,1)}), bf16[2,256,1536]{2,1,0:T(8,128)(2,1)}, u32[]{:S(2)}, u32[]{:S(2)}) async-start(bf16[2,256,1536]{2,1,0:T(8,128)(2,1)} %pad_maximum_fusion.2), calls=%async_computation.1 | async-start | bytes 3145728 | tf_op jit(solution)/shard_map/all_to_all | solution.py:607
  254.8 2.3 copy-done.3
  260.8 28.9 %collective-permute-done.8.refs_1_ = bf16[2,48,3072]{2,1,0:T(8,128)(2,1)} collective-permute-done((bf16[2,48,3072]{2,1,0:T(8,128)(2,1)}, bf16[2,48,3072]{2,1,0:T(8,128)(2,1)}, u32[]{:S(2)}, u32[]{:S(2)}) %collective-permute-start.8) | collective-permute-done | bytes 589856 | tf_op jit(solution)/shard_map/ppermute | solution.py:515
  289.7 1.5 tile_sums.25
  291.1 4.6 %collective-permute-start.9 = (bf16[2,48,3072]{2,1,0:T(8,128)(2,1)S(1)}, bf16[2,48,3072]{2,1,0:T(8,128)(2,1)S(1)}, u32[]{:S(2)}, u32[]{:S(2)}) collective-permute-start(bf16[2,48,3072]{2,1,0:T(8,128)(2,1)S(1)} %tile_sums.25), channel_id=1, source_target_pairs={{0,8},{2,10},{4,12},{6,14},{8,16},{10,18},{12,20},{14,22},{16,24},... | collective-permute-start | bytes 1769480 | tf_op jit(solution)/shard_map/ppermute | solution.py:515
  295.8 4.2 %collective-permute-done.12.refs_2_ = bf16[2,48,3072]{2,1,0:T(8,128)(2,1)S(1)} collective-permute-done((bf16[2,48,3072]{2,1,0:T(8,128)(2,1)S(1)}, bf16[2,48,3072]{2,1,0:T(8,128)(2,1)S(1)}, u32[]{:S(2)}, u32[]{:S(2)}) %collective-permute-start.12) | collective-permute-done | bytes 589856 | tf_op jit(solution)/shard_map/ppermute | solution.py:515
  300.0 7.5 %collective-permute-done.9.refs_1_ = bf16[2,48,3072]{2,1,0:T(8,128)(2,1)S(1)} collective-permute-done((bf16[2,48,3072]{2,1,0:T(8,128)(2,1)S(1)}, bf16[2,48,3072]{2,1,0:T(8,128)(2,1)S(1)}, u32[]{:S(2)}, u32[]{:S(2)}) %collective-permute-start.9) | collective-permute-done | bytes 589856 | tf_op jit(solution)/shard_map/ppermute | solution.py:515
  307.5 1.7 tile_sums.29
  310.0 3.2 tile_sums.36
  313.2 3.0 fusion.7
  316.2 1.8 convolution_convert_fusion.1
  318.0 4.9 %all-to-all-start.2 = ((bf16[32,16,512]{2,1,0:T(8,128)(2,1)}), bf16[32,16,512]{2,1,0:T(8,128)(2,1)}, u32[]{:S(2)}, u32[]{:S(2)}) async-start(bf16[32,16,512]{2,1,0:T(8,128)(2,1)} %bitcast.37), calls=%async_computation.2 | async-start | bytes 1048576 | tf_op jit(solution)/shard_map/all_to_all | solution.py:618
  322.9 1.7 constant_dynamic-update-slice_fusion.1
  324.6 1.7 constant_dynamic-update-slice_fusion.3
  326.3 16.0 %collective-permute-done.19.refs_2_ = bf16[2,80,3072]{2,1,0:T(8,128)(2,1)} collective-permute-done((bf16[2,80,3072]{2,1,0:T(8,128)(2,1)}, bf16[2,80,3072]{2,1,0:T(8,128)(2,1)}, u32[]{:S(2)}, u32[]{:S(2)}) %collective-permute-start.19) | collective-permute-done | bytes 983072 | tf_op jit(solution)/shard_map/ppermute | solution.py:515
  342.3 2.3 copy-done.4
  344.7 3.5 tile_sums.37
  348.2 2.2 convolution_convert_fusion
  353.1 3.5 all-to-all-start.3
  359.2 12.4 %all-to-all-done.3 = bf16[32,16,512]{2,1,0:T(8,128)(2,1)S(1)} async-done(((bf16[32,16,512]{2,1,0:T(8,128)(2,1)}), bf16[32,16,512]{2,1,0:T(8,128)(2,1)S(1)}, u32[]{:S(2)}, u32[]{:S(2)}) %all-to-all-start.3) | async-done | bytes 524320 | tf_op jit(solution)/shard_map/all_to_all | solution.py:622
  (144 shorter events, 39.9 us)
Async XLA Ops:
  0.6 5.1 %copy-start = (bf16[1536,512]{1,0:T(8,128)(2,1)S(1)}, bf16[1536,512]{1,0:T(8,128)(2,1)}, u32[]{:S(2)}) copy-start(bf16[1536,512]{1,0:T(8,128)(2,1)} %param.10) | copy-start | bytes 4718596
  0.6 3.1 copy-start.35
  0.7 3.0 copy-start.34
  3.2 2.6 copy-start.29
  3.2 10.3 %collective-permute-start.22 = (bf16[128,3072]{1,0:T(8,128)(2,1)S(1)}, bf16[128,3072]{1,0:T(8,128)(2,1)S(1)}, u32[]{:S(2)}, u32[]{:S(2)}) collective-permute-start(bf16[128,3072]{1,0:T(8,128)(2,1)S(1)} %get-tuple-element.18), channel_id=1, source_target_pairs={{0,2},{2,0},{4,6},{6,4},{8,10},{10,8},{12,14},{14,12},{16,18},{18,... | collective-permute-start | bytes 2359304 | tf_op jit(solution)/shard_map/ppermute | solution.py:515
  3.7 60.4 %collective-permute-start.2 = (bf16[72,128,128]{2,1,0:T(8,128)(2,1)}, bf16[72,128,128]{2,1,0:T(8,128)(2,1)}, u32[]{:S(2)}, u32[]{:S(2)}) collective-permute-start(bf16[72,128,128]{2,1,0:T(8,128)(2,1)} %tiles_own.9), channel_id=1, source_target_pairs={{0,2},{2,0},{4,6},{6,4},{8,10},{10,8},{12,14},{14,12},{16,18},{18,... | collective-permute-start | bytes 7077896 | tf_op jit(solution)/shard_map/ppermute | solution.py:515
  8.7 4.8 %copy-start.31 = (s32[72,1]{0,1:T(1,128)S(1)}, s32[72,1]{0,1:T(1,128)}, u32[]{:S(2)}) copy-start(s32[72,1]{0,1:T(1,128)} %param.15) | copy-start | bytes 868
  8.7 25.8 %all-to-all-start = ((bf16[2,256,1536]{2,1,0:T(8,128)(2,1)}), bf16[2,256,1536]{2,1,0:T(8,128)(2,1)}, u32[]{:S(2)}, u32[]{:S(2)}) async-start(bf16[2,256,1536]{2,1,0:T(8,128)(2,1)} %bitcast.7), calls=%async_computation | async-start | bytes 3145728 | tf_op jit(solution)/shard_map/all_to_all | solution.py:553
  13.5 10.0 %copy-start.32 = (s32[72]{0:T(128)S(1)}, s32[72]{0:T(128)}, u32[]{:S(2)}) copy-start(s32[72]{0:T(128)} %param.17) | copy-start | bytes 868
  13.5 9.9 %copy-start.33 = (s32[72]{0:T(128)S(1)}, s32[72]{0:T(128)}, u32[]{:S(2)}) copy-start(s32[72]{0:T(128)} %param.16) | copy-start | bytes 868
  16.0 38.8 %collective-permute-start.23 = (bf16[2,128,3072]{2,1,0:T(8,128)(2,1)S(1)}, bf16[2,128,3072]{2,1,0:T(8,128)(2,1)}, u32[]{:S(2)}, u32[]{:S(2)}) collective-permute-start(bf16[2,128,3072]{2,1,0:T(8,128)(2,1)S(1)} %pad_maximum_fusion.1.refs_0_), channel_id=1, source_target_pairs={{0,8},{2,10},{4,12},{6,14},{8,16},{10,18},{12,20},{14,22},{16,24},... | collective-permute-start | bytes 4718600 | tf_op jit(solution)/shard_map/ppermute | solution.py:515
  22.1 38.0 %collective-permute-start.26 = (bf16[2,128,3072]{2,1,0:T(8,128)(2,1)S(1)}, bf16[2,128,3072]{2,1,0:T(8,128)(2,1)}, u32[]{:S(2)}, u32[]{:S(2)}) collective-permute-start(bf16[2,128,3072]{2,1,0:T(8,128)(2,1)S(1)} %pad_maximum_fusion.1.refs_0_), channel_id=1, source_target_pairs={{8,0},{10,2},{12,4},{14,6},{16,8},{18,10},{20,12},{22,14},{24,16},... | collective-permute-start | bytes 4718600 | tf_op jit(solution)/shard_map/ppermute | solution.py:515
  24.1 12.7 %collective-permute-start = (s32[298]{0:T(512)S(1)}, s32[298]{0:T(512)S(1)}, u32[]{:S(2)}, u32[]{:S(2)}) collective-permute-start(s32[298]{0:T(512)S(1)} %pad_add_fusion.1.meta_own), channel_id=1, source_target_pairs={{0,2},{2,0},{4,6},{6,4},{8,10},{10,8},{12,14},{14,12},{16,18},{18,... | collective-permute-start | bytes 3584 | tf_op jit(solution)/shard_map/ppermute | solution.py:515
  24.1 57.1 %collective-permute-start.33 = (bf16[2,128,3072]{2,1,0:T(8,128)(2,1)S(1)}, bf16[2,128,3072]{2,1,0:T(8,128)(2,1)}, u32[]{:S(2)}, u32[]{:S(2)}) collective-permute-start(bf16[2,128,3072]{2,1,0:T(8,128)(2,1)S(1)} %pad_maximum_fusion.1.refs_0_), channel_id=1, source_target_pairs={{0,4},{2,6},{4,0},{6,2},{8,12},{10,14},{12,8},{14,10},{16,20},{18,... | collective-permute-start | bytes 4718600 | tf_op jit(solution)/shard_map/ppermute | solution.py:515
  36.8 24.6 %collective-permute-start.1 = (bf16[2,128,1536]{2,1,0:T(8,128)(2,1)S(1)}, bf16[2,128,1536]{2,1,0:T(8,128)(2,1)S(1)}, u32[]{:S(2)}, u32[]{:S(2)}) collective-permute-start(bf16[2,128,1536]{2,1,0:T(8,128)(2,1)S(1)} %get-tuple-element.21), channel_id=1, source_target_pairs={{0,2},{2,0},{4,6},{6,4},{8,10},{10,8},{12,14},{14,12},{16,18},{18,... | collective-permute-start | bytes 2359304 | tf_op jit(solution)/shard_map/ppermute | solution.py:515
  54.7 28.4 %collective-permute-start.24 = (bf16[2,128,3072]{2,1,0:T(8,128)(2,1)}, bf16[2,128,3072]{2,1,0:T(8,128)(2,1)}, u32[]{:S(2)}, u32[]{:S(2)}) collective-permute-start(bf16[2,128,3072]{2,1,0:T(8,128)(2,1)} %collective-permute-done.23.refs_1_), channel_id=1, source_target_pairs={{8,16},{10,18},{12,20},{14,22},{16,24},{18,26},{20,28},{22,30},{9,... | collective-permute-start | bytes 4718600 | tf_op jit(solution)/shard_map/ppermute | solution.py:515
  60.1 37.5 %collective-permute-start.27 = (bf16[2,128,3072]{2,1,0:T(8,128)(2,1)}, bf16[2,128,3072]{2,1,0:T(8,128)(2,1)}, u32[]{:S(2)}, u32[]{:S(2)}) collective-permute-start(bf16[2,128,3072]{2,1,0:T(8,128)(2,1)} %collective-permute-done.26.refs_2_), channel_id=1, source_target_pairs={{8,0},{10,2},{12,4},{14,6},{16,8},{18,10},{20,12},{22,14},{9,1},{1... | collective-permute-start | bytes 4718600 | tf_op jit(solution)/shard_map/ppermute | solution.py:515
  62.3 36.0 %collective-permute-start.34 = (bf16[2,128,3072]{2,1,0:T(8,128)(2,1)}, bf16[2,128,3072]{2,1,0:T(8,128)(2,1)}, u32[]{:S(2)}, u32[]{:S(2)}) collective-permute-start(bf16[2,128,3072]{2,1,0:T(8,128)(2,1)} %collective-permute-done.23.refs_1_), channel_id=1, source_target_pairs={{8,12},{10,14},{12,8},{14,10},{16,20},{18,22},{20,16},{22,18},{24,... | collective-permute-start | bytes 4718600 | tf_op jit(solution)/shard_map/ppermute | solution.py:515
  64.1 37.4 %collective-permute-start.35 = (bf16[2,128,3072]{2,1,0:T(8,128)(2,1)}, bf16[2,128,3072]{2,1,0:T(8,128)(2,1)}, u32[]{:S(2)}, u32[]{:S(2)}) collective-permute-start(bf16[2,128,3072]{2,1,0:T(8,128)(2,1)} %collective-permute-done.26.refs_2_), channel_id=1, source_target_pairs={{0,4},{2,6},{4,0},{6,2},{8,12},{10,14},{12,8},{14,10},{16,20},{18,... | collective-permute-start | bytes 4718600 | tf_op jit(solution)/shard_map/ppermute | solution.py:515
  80.5 144.9 %copy-start.1 = (bf16[2,72,128,128]{3,2,1,0:T(8,128)(2,1)}, bf16[2,72,128,128]{3,2,1,0:T(8,128)(2,1)S(1)}, u32[]{:S(2)}) copy-start(bf16[2,72,128,128]{3,2,1,0:T(8,128)(2,1)S(1)} %tile_parts.1.parts) | copy-start | bytes 14155780
  81.2 21.0 %collective-permute-start.16 = (bf16[2,2,80,3072]{3,2,1,0:T(8,128)(2,1)S(1)}, bf16[2,2,80,3072]{3,2,1,0:T(8,128)(2,1)S(1)}, u32[]{:S(2)}, u32[]{:S(2)}) collective-permute-start(bf16[2,2,80,3072]{3,2,1,0:T(8,128)(2,1)S(1)} %tile_sums.33), channel_id=1, source_target_pairs={{24,16},{26,18},{28,20},{30,22},{25,17},{27,19},{29,21},{31,23}} | collective-permute-start | bytes 5898248 | tf_op jit(solution)/shard_map/ppermute | solution.py:515
  83.1 53.4 %collective-permute-start.13 = (bf16[2,2,80,3072]{3,2,1,0:T(8,128)(2,1)S(1)}, bf16[2,2,80,3072]{3,2,1,0:T(8,128)(2,1)S(1)}, u32[]{:S(2)}, u32[]{:S(2)}) collective-permute-start(bf16[2,2,80,3072]{3,2,1,0:T(8,128)(2,1)S(1)} %tile_sums.30), channel_id=1, source_target_pairs={{0,8},{2,10},{4,12},{6,14},{1,9},{3,11},{5,13},{7,15}} | collective-permute-start | bytes 5898248 | tf_op jit(solution)/shard_map/ppermute | solution.py:515
  97.6 8.1 %collective-permute-start.29 = (bf16[2,128,3072]{2,1,0:T(8,128)(2,1)}, bf16[2,128,3072]{2,1,0:T(8,128)(2,1)S(1)}, u32[]{:S(2)}, u32[]{:S(2)}) collective-permute-start(bf16[2,128,3072]{2,1,0:T(8,128)(2,1)} %collective-permute-done.24.refs_0_), channel_id=1, source_target_pairs={{16,24},{18,26},{20,28},{22,30},{17,25},{19,27},{21,29},{23,31}} | collective-permute-start | bytes 4718600 | tf_op jit(solution)/shard_map/ppermute | solution.py:515
  98.4 38.9 %collective-permute-start.31 = (bf16[2,128,3072]{2,1,0:T(8,128)(2,1)}, bf16[2,128,3072]{2,1,0:T(8,128)(2,1)S(1)}, u32[]{:S(2)}, u32[]{:S(2)}) collective-permute-start(bf16[2,128,3072]{2,1,0:T(8,128)(2,1)} %collective-permute-done.27.refs_1_), channel_id=1, source_target_pairs={{8,0},{10,2},{12,4},{14,6},{9,1},{11,3},{13,5},{15,7}} | collective-permute-start | bytes 4718600 | tf_op jit(solution)/shard_map/ppermute | solution.py:515
  101.5 42.0 %collective-permute-start.25 = (bf16[2,128,3072]{2,1,0:T(8,128)(2,1)}, bf16[2,128,3072]{2,1,0:T(8,128)(2,1)S(1)}, u32[]{:S(2)}, u32[]{:S(2)}) collective-permute-start(bf16[2,128,3072]{2,1,0:T(8,128)(2,1)} %collective-permute-done.24.refs_0_), channel_id=1, source_target_pairs={{16,20},{18,22},{20,16},{22,18},{24,28},{26,30},{28,24},{30,26},{1... | collective-permute-start | bytes 4718600 | tf_op jit(solution)/shard_map/ppermute | solution.py:515
  102.3 48.6 %collective-permute-start.28 = (bf16[2,128,3072]{2,1,0:T(8,128)(2,1)}, bf16[2,128,3072]{2,1,0:T(8,128)(2,1)S(1)}, u32[]{:S(2)}, u32[]{:S(2)}) collective-permute-start(bf16[2,128,3072]{2,1,0:T(8,128)(2,1)} %collective-permute-done.27.refs_1_), channel_id=1, source_target_pairs={{0,4},{2,6},{4,0},{6,2},{8,12},{10,14},{12,8},{14,10},{1,5},{3,7},... | collective-permute-start | bytes 4718600 | tf_op jit(solution)/shard_map/ppermute | solution.py:515
  105.7 47.5 %collective-permute-start.30 = (bf16[2,128,3072]{2,1,0:T(8,128)(2,1)S(1)}, bf16[2,128,3072]{2,1,0:T(8,128)(2,1)S(1)}, u32[]{:S(2)}, u32[]{:S(2)}) collective-permute-start(bf16[2,128,3072]{2,1,0:T(8,128)(2,1)S(1)} %collective-permute-done.29.refs_2_), channel_id=1, source_target_pairs={{24,28},{26,30},{28,24},{30,26},{25,29},{27,31},{29,25},{31,27}} | collective-permute-start | bytes 4718600 | tf_op jit(solution)/shard_map/ppermute | solution.py:515
  136.5 73.5 %collective-permute-start.17 = (bf16[2,2,80,3072]{3,2,1,0:T(8,128)(2,1)S(1)}, bf16[2,2,80,3072]{3,2,1,0:T(8,128)(2,1)S(1)}, u32[]{:S(2)}, u32[]{:S(2)}) collective-permute-start(bf16[2,2,80,3072]{3,2,1,0:T(8,128)(2,1)S(1)} %tile_sums.34), channel_id=1, source_target_pairs={{16,8},{18,10},{20,12},{22,14},{24,16},{26,18},{28,20},{30,22},{17... | collective-permute-start | bytes 5898248 | tf_op jit(solution)/shard_map/ppermute | solution.py:515
  137.3 39.2 %collective-permute-start.32 = (bf16[2,128,3072]{2,1,0:T(8,128)(2,1)S(1)}, bf16[2,128,3072]{2,1,0:T(8,128)(2,1)S(1)}, u32[]{:S(2)}, u32[]{:S(2)}) collective-permute-start(bf16[2,128,3072]{2,1,0:T(8,128)(2,1)S(1)} %collective-permute-done.31.refs_3_), channel_id=1, source_target_pairs={{0,4},{2,6},{4,0},{6,2},{1,5},{3,7},{5,1},{7,3}} | collective-permute-start | bytes 4718600 | tf_op jit(solution)/shard_map/ppermute | solution.py:515
  143.5 7.3 %copy-start.12 = (bf16[2,128,3072]{2,1,0:T(8,128)(2,1)}, bf16[2,128,3072]{2,1,0:T(8,128)(2,1)S(1)}, u32[]{:S(2)}) copy-start(bf16[2,128,3072]{2,1,0:T(8,128)(2,1)S(1)} %collective-permute-done.25.refs_0_) | copy-start | bytes 4718596
  143.5 80.5 %collective-permute-start.14 = (bf16[2,2,80,3072]{3,2,1,0:T(8,128)(2,1)}, bf16[2,2,80,3072]{3,2,1,0:T(8,128)(2,1)}, u32[]{:S(2)}, u32[]{:S(2)}) collective-permute-start(bf16[2,2,80,3072]{3,2,1,0:T(8,128)(2,1)} %tile_sums.31), channel_id=1, source_target_pairs={{0,8},{2,10},{4,12},{6,14},{8,16},{10,18},{12,20},{14,22},{1,9},{3... | collective-permute-start | bytes 5898248 | tf_op jit(solution)/shard_map/ppermute | solution.py:515
  150.9 2.3 copy-start.14
  150.9 54.5 %collective-permute-start.4 = (bf16[2,48,3072]{2,1,0:T(8,128)(2,1)}, bf16[2,48,3072]{2,1,0:T(8,128)(2,1)S(1)}, u32[]{:S(2)}, u32[]{:S(2)}) collective-permute-start(bf16[2,48,3072]{2,1,0:T(8,128)(2,1)} %tile_sums.20), channel_id=1, source_target_pairs={{0,4},{2,6},{4,0},{6,2},{8,12},{10,14},{12,8},{14,10},{16,20},{18,... | collective-permute-start | bytes 1769480 | tf_op jit(solution)/shard_map/ppermute | solution.py:515
  154.3 52.6 %collective-permute-start.6 = (bf16[2,48,3072]{2,1,0:T(8,128)(2,1)}, bf16[2,48,3072]{2,1,0:T(8,128)(2,1)S(1)}, u32[]{:S(2)}, u32[]{:S(2)}) collective-permute-start(bf16[2,48,3072]{2,1,0:T(8,128)(2,1)} %tile_sums.22), channel_id=1, source_target_pairs={{0,4},{2,6},{4,0},{6,2},{8,12},{10,14},{12,8},{14,10},{16,20},{18,... | collective-permute-start | bytes 1769480 | tf_op jit(solution)/shard_map/ppermute | solution.py:515
  177.6 51.1 %collective-permute-start.5 = (bf16[2,48,3072]{2,1,0:T(8,128)(2,1)}, bf16[2,48,3072]{2,1,0:T(8,128)(2,1)S(1)}, u32[]{:S(2)}, u32[]{:S(2)}) collective-permute-start(bf16[2,48,3072]{2,1,0:T(8,128)(2,1)} %tile_sums.21), channel_id=1, source_target_pairs={{0,4},{2,6},{4,0},{6,2},{8,12},{10,14},{12,8},{14,10},{16,20},{18,... | collective-permute-start | bytes 1769480 | tf_op jit(solution)/shard_map/ppermute | solution.py:515
  190.3 6.4 %copy-start.13 = (bf16[2,128,3072]{2,1,0:T(8,128)(2,1)S(1)}, bf16[2,128,3072]{2,1,0:T(8,128)(2,1)}, u32[]{:S(2)}) copy-start(bf16[2,128,3072]{2,1,0:T(8,128)(2,1)} %copy-done.12) | copy-start | bytes 4718596
  190.3 6.4 %copy-start.19 = (bf16[2,128,3072]{2,1,0:T(8,128)(2,1)S(1)}, bf16[2,128,3072]{2,1,0:T(8,128)(2,1)}, u32[]{:S(2)}) copy-start(bf16[2,128,3072]{2,1,0:T(8,128)(2,1)} %copy-done.18) | copy-start | bytes 4718596
  205.4 1.5 copy-start.22
  205.4 42.2 %collective-permute-start.36 = (bf16[2,128,1536]{2,1,0:T(8,128)(2,1)}, bf16[2,128,1536]{2,1,0:T(8,128)(2,1)}, u32[]{:S(2)}, u32[]{:S(2)}) collective-permute-start(bf16[2,128,1536]{2,1,0:T(8,128)(2,1)} %get-tuple-element.14), channel_id=1, source_target_pairs={{0,2},{2,0},{4,6},{6,4},{8,10},{10,8},{12,14},{14,12},{16,18},{18,... | collective-permute-start | bytes 2359304 | tf_op jit(solution)/shard_map/ppermute | solution.py:515
  206.9 3.1 copy-start.10
  206.9 28.9 %collective-permute-start.10 = (bf16[2,48,3072]{2,1,0:T(8,128)(2,1)}, bf16[2,48,3072]{2,1,0:T(8,128)(2,1)}, u32[]{:S(2)}, u32[]{:S(2)}) collective-permute-start(bf16[2,48,3072]{2,1,0:T(8,128)(2,1)} %tile_sums.26), channel_id=1, source_target_pairs={{24,16},{26,18},{28,20},{30,22},{25,17},{27,19},{29,21},{31,23}} | collective-permute-start | bytes 1769480 | tf_op jit(solution)/shard_map/ppermute | solution.py:515
  210.0 33.0 %collective-permute-start.7 = (bf16[2,48,3072]{2,1,0:T(8,128)(2,1)}, bf16[2,48,3072]{2,1,0:T(8,128)(2,1)}, u32[]{:S(2)}, u32[]{:S(2)}) collective-permute-start(bf16[2,48,3072]{2,1,0:T(8,128)(2,1)} %tile_sums.23), channel_id=1, source_target_pairs={{0,8},{2,10},{4,12},{6,14},{1,9},{3,11},{5,13},{7,15}} | collective-permute-start | bytes 1769480 | tf_op jit(solution)/shard_map/ppermute | solution.py:515
  224.1 86.0 %collective-permute-start.18 = (bf16[2,2,80,3072]{3,2,1,0:T(8,128)(2,1)}, bf16[2,2,80,3072]{3,2,1,0:T(8,128)(2,1)S(1)}, u32[]{:S(2)}, u32[]{:S(2)}) collective-permute-start(bf16[2,2,80,3072]{3,2,1,0:T(8,128)(2,1)} %tile_sums.35), channel_id=1, source_target_pairs={{8,0},{10,2},{12,4},{14,6},{16,8},{18,10},{20,12},{22,14},{24,16},... | collective-permute-start | bytes 5898248 | tf_op jit(solution)/shard_map/ppermute | solution.py:515
  229.6 80.4 %collective-permute-start.15 = (bf16[2,2,80,3072]{3,2,1,0:T(8,128)(2,1)}, bf16[2,2,80,3072]{3,2,1,0:T(8,128)(2,1)}, u32[]{:S(2)}, u32[]{:S(2)}) collective-permute-start(bf16[2,2,80,3072]{3,2,1,0:T(8,128)(2,1)} %tile_sums.32), channel_id=1, source_target_pairs={{0,8},{2,10},{4,12},{6,14},{8,16},{10,18},{12,20},{14,22},{16,24},... | collective-permute-start | bytes 5898248 | tf_op jit(solution)/shard_map/ppermute | solution.py:515
  235.9 2.3 copy-start.2
  241.3 6.2 %copy-start.23 = (bf16[2,128,1536]{2,1,0:T(8,128)(2,1)S(1)}, bf16[2,128,1536]{2,1,0:T(8,128)(2,1)}, u32[]{:S(2)}) copy-start(bf16[2,128,1536]{2,1,0:T(8,128)(2,1)} %copy-done.22) | copy-start | bytes 2359300
  241.3 16.8 %collective-permute-start.11 = (bf16[2,48,3072]{2,1,0:T(8,128)(2,1)}, bf16[2,48,3072]{2,1,0:T(8,128)(2,1)}, u32[]{:S(2)}, u32[]{:S(2)}) collective-permute-start(bf16[2,48,3072]{2,1,0:T(8,128)(2,1)} %tile_sums.27), channel_id=1, source_target_pairs={{16,8},{18,10},{20,12},{22,14},{24,16},{26,18},{28,20},{30,22},{17... | collective-permute-start | bytes 1769480 | tf_op jit(solution)/shard_map/ppermute | solution.py:515
  245.4 44.2 %collective-permute-start.8 = (bf16[2,48,3072]{2,1,0:T(8,128)(2,1)}, bf16[2,48,3072]{2,1,0:T(8,128)(2,1)}, u32[]{:S(2)}, u32[]{:S(2)}) collective-permute-start(bf16[2,48,3072]{2,1,0:T(8,128)(2,1)} %tile_sums.24), channel_id=1, source_target_pairs={{0,8},{2,10},{4,12},{6,14},{8,16},{10,18},{12,20},{14,22},{1,9},{3... | collective-permute-start | bytes 1769480 | tf_op jit(solution)/shard_map/ppermute | solution.py:515
  250.1 63.0 %all-to-all-start.1 = ((bf16[2,256,1536]{2,1,0:T(8,128)(2,1)}), bf16[2,256,1536]{2,1,0:T(8,128)(2,1)}, u32[]{:S(2)}, u32[]{:S(2)}) async-start(bf16[2,256,1536]{2,1,0:T(8,128)(2,1)} %pad_maximum_fusion.2), calls=%async_computation.1 | async-start | bytes 3145728 | tf_op jit(solution)/shard_map/all_to_all | solution.py:607
  254.8 2.3 copy-start.3
  258.0 31.6 %copy-start.9 = (bf16[2,48,3072]{2,1,0:T(8,128)(2,1)S(1)}, bf16[2,48,3072]{2,1,0:T(8,128)(2,1)}, u32[]{:S(2)}) copy-start(bf16[2,48,3072]{2,1,0:T(8,128)(2,1)} %copy-done.8) | copy-start | bytes 1769476
  258.0 37.7 %collective-permute-start.3 = (bf16[2,48,3072]{2,1,0:T(8,128)(2,1)S(1)}, bf16[2,48,3072]{2,1,0:T(8,128)(2,1)S(1)}, u32[]{:S(2)}, u32[]{:S(2)}) collective-permute-start(bf16[2,48,3072]{2,1,0:T(8,128)(2,1)S(1)} %tile_sums.19), channel_id=1, source_target_pairs={{0,4},{2,6},{4,0},{6,2},{8,12},{10,14},{12,8},{14,10},{16,20},{18,... | collective-permute-start | bytes 1769480 | tf_op jit(solution)/shard_map/ppermute | solution.py:515
  259.5 40.5 %collective-permute-start.12 = (bf16[2,48,3072]{2,1,0:T(8,128)(2,1)S(1)}, bf16[2,48,3072]{2,1,0:T(8,128)(2,1)S(1)}, u32[]{:S(2)}, u32[]{:S(2)}) collective-permute-start(bf16[2,48,3072]{2,1,0:T(8,128)(2,1)S(1)} %tile_sums.28), channel_id=1, source_target_pairs={{8,0},{10,2},{12,4},{14,6},{16,8},{18,10},{20,12},{22,14},{24,16},... | collective-permute-start | bytes 1769480 | tf_op jit(solution)/shard_map/ppermute | solution.py:515
  291.1 16.4 %collective-permute-start.9 = (bf16[2,48,3072]{2,1,0:T(8,128)(2,1)S(1)}, bf16[2,48,3072]{2,1,0:T(8,128)(2,1)S(1)}, u32[]{:S(2)}, u32[]{:S(2)}) collective-permute-start(bf16[2,48,3072]{2,1,0:T(8,128)(2,1)S(1)} %tile_sums.25), channel_id=1, source_target_pairs={{0,8},{2,10},{4,12},{6,14},{8,16},{10,18},{12,20},{14,22},{16,24},... | collective-permute-start | bytes 1769480 | tf_op jit(solution)/shard_map/ppermute | solution.py:515
  310.0 14.6 %collective-permute-start.20 = (bf16[48,3072]{1,0:T(8,128)(2,1)}, bf16[48,3072]{1,0:T(8,128)(2,1)}, u32[]{:S(2)}, u32[]{:S(2)}) collective-permute-start(bf16[48,3072]{1,0:T(8,128)(2,1)} %get-tuple-element.11), channel_id=1, source_target_pairs={{0,2},{2,0},{4,6},{6,4},{8,10},{10,8},{12,14},{14,12},{16,18},{18,... | collective-permute-start | bytes 884744 | tf_op jit(solution)/shard_map/ppermute | solution.py:515
  313.2 29.2 %collective-permute-start.19 = (bf16[2,80,3072]{2,1,0:T(8,128)(2,1)}, bf16[2,80,3072]{2,1,0:T(8,128)(2,1)}, u32[]{:S(2)}, u32[]{:S(2)}) collective-permute-start(bf16[2,80,3072]{2,1,0:T(8,128)(2,1)} %tile_sums.36), channel_id=1, source_target_pairs={{0,4},{2,6},{4,0},{6,2},{8,12},{10,14},{12,8},{14,10},{16,20},{18,... | collective-permute-start | bytes 2949128 | tf_op jit(solution)/shard_map/ppermute | solution.py:515
  316.2 1.8 copy-start.25
  318.0 33.1 %all-to-all-start.2 = ((bf16[32,16,512]{2,1,0:T(8,128)(2,1)}), bf16[32,16,512]{2,1,0:T(8,128)(2,1)}, u32[]{:S(2)}, u32[]{:S(2)}) async-start(bf16[32,16,512]{2,1,0:T(8,128)(2,1)} %bitcast.37), calls=%async_computation.2 | async-start | bytes 1048576 | tf_op jit(solution)/shard_map/all_to_all | solution.py:618
  342.3 2.3 copy-start.4
  344.7 3.5 copy-start.26
  344.7 3.5 copy-start.30
  348.2 8.5 %collective-permute-start.21 = (bf16[80,3072]{1,0:T(8,128)(2,1)}, bf16[80,3072]{1,0:T(8,128)(2,1)S(1)}, u32[]{:S(2)}, u32[]{:S(2)}) collective-permute-start(bf16[80,3072]{1,0:T(8,128)(2,1)} %get-tuple-element.12), channel_id=1, source_target_pairs={{0,2},{2,0},{4,6},{6,4},{8,10},{10,8},{12,14},{14,12},{16,18},{18,... | collective-permute-start | bytes 1474568 | tf_op jit(solution)/shard_map/ppermute | solution.py:515
  350.3 6.3 %copy-start.27 = (bf16[128,3072]{1,0:T(8,128)(2,1)S(1)}, bf16[128,3072]{1,0:T(8,128)(2,1)}, u32[]{:S(2)}) copy-start(bf16[128,3072]{1,0:T(8,128)(2,1)} %constant_dynamic-update-slice_fusion.3) | copy-start | bytes 2359300
  353.1 18.5 %all-to-all-start.3 = ((bf16[32,16,512]{2,1,0:T(8,128)(2,1)}), bf16[32,16,512]{2,1,0:T(8,128)(2,1)S(1)}, u32[]{:S(2)}, u32[]{:S(2)}) async-start(bf16[32,16,512]{2,1,0:T(8,128)(2,1)} %broadcast_in_dim.2), calls=%async_computation.3 | async-start | bytes 1048576 | tf_op jit(solution)/shard_map/all_to_all | solution.py:622
  (13 other events, 14.4 us)
where the time goes:
time: 375 us; the launch traced here: 372 us
  waiting for transfers between devices  151 us (40%)
  starting transfers between devices  101 us (27%)
  Pallas kernels  68.9 us (18%)
  local copies, waits for them, and re-layouts  30.5 us (8%)
  other arithmetic  11.3 us (3%)
  matrix products  8.96 us (2%)
    ppermute x37, waiting for transfers between devices, permute(): return lax.ppermute(a, 'row', pairs)  130 us
    ppermute x37, starting transfers between devices, permute(): return lax.ppermute(a, 'row', pairs)  82.8 us
    pallas_call x19, Pallas kernels, tile_sums(): pl.pallas_call(functools.partial(sum_kernel, spec), out_shape=out, in_spe...  35.5 us
    pallas_call x4, Pallas kernels, grad_sums(): pl.pallas_call(functools.partial(grad_kernel, (tuple(chips), bool(sums),...  23.4 us
    unnamed x75, local copies, waits for them, and re-layouts  23.1 us
    all_to_all x1, waiting for transfers between devices, finish(): lax.all_to_all(jnp.broadcast_to(share[None], (devices,) + share.shape), a...  12.4 us
    pallas_call x1, Pallas kernels, tile_parts(): pl.pallas_call(parts_kernel, out_shape=jax.ShapeDtypeStruct((2, count, fe...  9.97 us
    all_to_all x1, waiting for transfers between devices, grid_device(): lax.all_to_all(msg_t.reshape(col_count, feats, nodes), 'col', split_axis=...  8.79 us
  transfers between devices with their start and end apart: 41, of which 12 were waited for; matrix products, arithmetic and copies ran while one was open for 8% of the time, Pallas kernels for 19%

commit v1 on v0

--- a/solution.py
+++ b/solution.py
@@ -588,16 +588,17 @@
         jnp.concatenate([keep_a, keep_b]), jnp.concatenate([other_a, other_b]), 0
     )
 
-    def grads(dx, steps, so_far, final=False):
-        arrays = [(line, across)[dx][dz] for dz in steps]
-        return grad_sums(env, [rel(dz, dx) for dz in steps], arrays, so_far, col_count, final)
-
-    near = [dz for dz in line if abs(dz) <= 1]
-    far = [dz for dz in line if abs(dz) > 1]
-    acc = grads(0, near, None)
-    acc = grads(0, far, acc)
-    acc = grads(1, near, acc)
-    own, send = grads(1, far, acc, True)
+    def grads(steps, so_far, final=False):
+        arrays = [(line, across)[dx][dz] for dx, dz in steps]
+        return grad_sums(env, [rel(dz, dx) for dx, dz in steps], arrays, so_far, col_count, final)
+
+    def both(dx, *steps):
+        return [(dx, sign * k) for k in steps for sign in (-1, 1)]
+
+    acc = grads([(0, 0)] + both(0, 1), None)
+    acc = grads([(1, 0)] + both(0, 2), acc)
+    acc = grads(both(1, 1) + both(0, *range(3, nz)), acc)
+    own, send = grads(both(1, *range(2, nz)), acc, True)
     dmsg = in_order(own, permute(send, swap), 1)
     return finish(node_feats, w_msg, pre_t, dmsg, aggregated)
 

time: 375 us -> 374 us (level)
    unnamed x75 -> x79, local copies, waits for them, and re-layouts: 23.1 us -> 22 us
where the time goes in v1:
time: 374 us; the launch traced here: 372 us
  waiting for transfers between devices  152 us (41%)
  starting transfers between devices  99.5 us (27%)
  Pallas kernels  69 us (18%)
  local copies, waits for them, and re-layouts  29.4 us (8%)
  other arithmetic  11.3 us (3%)
  matrix products  8.96 us (2%)
    ppermute x37, waiting for transfers between devices, permute(): return lax.ppermute(a, 'row', pairs)  131 us
    ppermute x37, starting transfers between devices, permute(): return lax.ppermute(a, 'row', pairs)  81.8 us
    pallas_call x19, Pallas kernels, tile_sums(): pl.pallas_call(functools.partial(sum_kernel, spec), out_shape=out, in_spe...  35.5 us
    pallas_call x4, Pallas kernels, grad_sums(): pl.pallas_call(functools.partial(grad_kernel, (tuple(chips), bool(sums),...  23.5 us
    unnamed x79, local copies, waits for them, and re-layouts  22 us
    all_to_all x1, waiting for transfers between devices, finish(): lax.all_to_all(jnp.broadcast_to(share[None], (devices,) + share.shape), a...  12.4 us
    pallas_call x1, Pallas kernels, tile_parts(): pl.pallas_call(parts_kernel, out_shape=jax.ShapeDtypeStruct((2, count, fe...  9.97 us
    all_to_all x1, waiting for transfers between devices, grid_device(): lax.all_to_all(msg_t.reshape(col_count, feats, nodes), 'col', split_axis=...  8.81 us
  transfers between devices with their start and end apart: 41, of which 12 were waited for; matrix products, arithmetic and copies ran while one was open for 8% of the time, Pallas kernels for 19%

profile of v1, /device:TPU:0, one launch (start us, length us, event | category | flops | bytes accessed | tf_op | source)
XLA Modules:
  0.0 371.5 jit_solution(3346440226606773527)
XLA Ops:
  0.7 2.5 dynamic-slice_bitcast_fusion
  3.7 2.1 fusion.1
  5.8 2.9 multiply_convert_fusion
  8.7 4.7 %all-to-all-start = ((bf16[2,256,1536]{2,1,0:T(8,128)(2,1)}), bf16[2,256,1536]{2,1,0:T(8,128)(2,1)}, u32[]{:S(2)}, u32[]{:S(2)}) async-start(bf16[2,256,1536]{2,1,0:T(8,128)(2,1)} %bitcast.7), calls=%async_computation | async-start | bytes 3145728 | tf_op jit(solution)/shard_map/all_to_all | solution.py:553
  14.4 1.5 pad_maximum_fusion.1.refs_0_
  15.9 6.1 %collective-permute-start.23 = (bf16[2,128,3072]{2,1,0:T(8,128)(2,1)S(1)}, bf16[2,128,3072]{2,1,0:T(8,128)(2,1)}, u32[]{:S(2)}, u32[]{:S(2)}) collective-permute-start(bf16[2,128,3072]{2,1,0:T(8,128)(2,1)S(1)} %pad_maximum_fusion.1.refs_0_), channel_id=1, source_target_pairs={{0,8},{2,10},{4,12},{6,14},{8,16},{10,18},{12,20},{14,22},{16,24},... | collective-permute-start | bytes 4718600 | tf_op jit(solution)/shard_map/ppermute | solution.py:515
  24.1 1.6 collective-permute-start.35
  25.6 8.8 %all-to-all-done = bf16[2,256,1536]{2,1,0:T(8,128)(2,1)} async-done(((bf16[2,256,1536]{2,1,0:T(8,128)(2,1)}), bf16[2,256,1536]{2,1,0:T(8,128)(2,1)}, u32[]{:S(2)}, u32[]{:S(2)}) %all-to-all-start) | async-done | bytes 1572896 | tf_op jit(solution)/shard_map/all_to_all | solution.py:553
  34.5 2.4 constant_dynamic-slice_fusion.1
  36.8 17.9 %collective-permute-done.23.refs_1_ = bf16[2,128,3072]{2,1,0:T(8,128)(2,1)} collective-permute-done((bf16[2,128,3072]{2,1,0:T(8,128)(2,1)S(1)}, bf16[2,128,3072]{2,1,0:T(8,128)(2,1)}, u32[]{:S(2)}, u32[]{:S(2)}) %collective-permute-start.23) | collective-permute-done | bytes 1572896 | tf_op jit(solution)/shard_map/ppermute | solution.py:515
  54.7 1.8 collective-permute-start.24
  56.5 3.5 collective-permute-done.26.refs_2_
  62.3 1.8 collective-permute-start.33
  64.1 3.4 collective-permute-start.34
  70.4 10.0 %tile_parts.1.parts = bf16[2,72,128,128]{3,2,1,0:T(8,128)(2,1)S(1)} custom-call(s32[298]{0:T(512)S(1)} %pad_add_fusion.1.meta_own, s32[298]{0:T(512)S(1)} %collective-permute-done.meta_other, bf16[2,128,1536]{2,1,0:T(8,128)(2,1)S(1)} %copy-done.5, bf16[2,128,1536]{2,1,0:T(8,128)(2,1)S(1)} %copy-done.23, bf16[72,128,128]{2,1,0:T(8,128)(2,1)} %tiles_own.9, ...), custom_call_target="tpu_custom_call" | custom-call | flops 1073741824 | bytes 12582912 | tf_op jit(solution)/shard_map/tile_parts/pallas_call | solution.py:323
  83.1 13.0 %collective-permute-start.13 = (bf16[2,2,80,3072]{3,2,1,0:T(8,128)(2,1)S(1)}, bf16[2,2,80,3072]{3,2,1,0:T(8,128)(2,1)S(1)}, u32[]{:S(2)}, u32[]{:S(2)}) collective-permute-start(bf16[2,2,80,3072]{3,2,1,0:T(8,128)(2,1)S(1)} %tile_sums.30), channel_id=1, source_target_pairs={{0,8},{2,10},{4,12},{6,14},{1,9},{3,11},{5,13},{7,15}} | collective-permute-start | bytes 5898248 | tf_op jit(solution)/shard_map/ppermute | solution.py:515
  96.1 1.5 collective-permute-done.27.refs_2_
  99.6 1.8 collective-permute-done.34.refs_1_
  102.2 3.4 collective-permute-start.28
  107.1 29.3 %collective-permute-done.13.refs_0_ = bf16[2,2,80,3072]{3,2,1,0:T(8,128)(2,1)S(1)} collective-permute-done((bf16[2,2,80,3072]{3,2,1,0:T(8,128)(2,1)S(1)}, bf16[2,2,80,3072]{3,2,1,0:T(8,128)(2,1)S(1)}, u32[]{:S(2)}, u32[]{:S(2)}) %collective-permute-start.13) | collective-permute-done | bytes 1966112 | tf_op jit(solution)/shard_map/ppermute | solution.py:515
  137.3 3.4 collective-permute-start.32
  140.7 2.8 tile_sums.31
  143.5 5.7 %collective-permute-start.14 = (bf16[2,2,80,3072]{3,2,1,0:T(8,128)(2,1)}, bf16[2,2,80,3072]{3,2,1,0:T(8,128)(2,1)}, u32[]{:S(2)}, u32[]{:S(2)}) collective-permute-start(bf16[2,2,80,3072]{3,2,1,0:T(8,128)(2,1)} %tile_sums.31), channel_id=1, source_target_pairs={{0,8},{2,10},{4,12},{6,14},{8,16},{10,18},{12,20},{14,22},{1,9},{3... | collective-permute-start | bytes 5898248 | tf_op jit(solution)/shard_map/ppermute | solution.py:515
  149.3 1.6 tile_sums.20
  151.6 1.6 tile_sums.22
  153.2 1.5 collective-permute-start.6
  154.7 1.8 tile_sums.21
  156.5 20.0 %collective-permute-done.32.refs_3_ = bf16[2,128,3072]{2,1,0:T(8,128)(2,1)S(1)} collective-permute-done((bf16[2,128,3072]{2,1,0:T(8,128)(2,1)S(1)}, bf16[2,128,3072]{2,1,0:T(8,128)(2,1)S(1)}, u32[]{:S(2)}, u32[]{:S(2)}) %collective-permute-start.32) | collective-permute-done | bytes 1572896 | tf_op jit(solution)/shard_map/ppermute | solution.py:515
  177.6 1.5 collective-permute-start.5
  179.1 5.4 %grad_sums.4.refs_3_ = f32[2,2,128,1536]{3,2,1,0:T(8,128)S(1)} custom-call(s32[23]{0:T(128)S(1)} %fusion.12.ids, s32[298]{0:T(512)S(1)} %pad_add_fusion.1.meta_own, s32[298]{0:T(512)S(1)} %collective-permute-done.meta_other, bf16[72,128,128]{2,1,0:T(8,128)(2,1)} %tiles_own.9, bf16[72,128,128]{2,1,0:T(8,128)(2,1)} %collective-permute-done.2.tiles_other, ...), custom_call_target="tpu_custom_call" | custom-call | flops 268435456 | bytes 8388608 | tf_op jit(solution)/shard_map/grad_sums/pallas_call | solution.py:438
  184.5 6.9 %grad_sums.5.refs_4_ = f32[2,2,128,1536]{3,2,1,0:T(8,128)S(1)} custom-call(s32[23]{0:T(128)S(1)} %fusion.12.ids, s32[298]{0:T(512)S(1)} %pad_add_fusion.1.meta_own, s32[298]{0:T(512)S(1)} %collective-permute-done.meta_other, bf16[72,128,128]{2,1,0:T(8,128)(2,1)} %tiles_own.9, bf16[72,128,128]{2,1,0:T(8,128)(2,1)} %collective-permute-done.2.tiles_other, ...), custom_call_target="tpu_custom_call" | custom-call | flops 268435456 | bytes 8388608 | tf_op jit(solution)/shard_map/grad_sums/pallas_call | solution.py:438
  191.4 5.3 %grad_sums.6.refs_4_ = f32[2,2,128,1536]{3,2,1,0:T(8,128)S(1)} custom-call(s32[23]{0:T(128)S(1)} %fusion.12.ids, s32[298]{0:T(512)S(1)} %pad_add_fusion.1.meta_own, s32[298]{0:T(512)S(1)} %collective-permute-done.meta_other, bf16[72,128,128]{2,1,0:T(8,128)(2,1)} %tiles_own.9, bf16[72,128,128]{2,1,0:T(8,128)(2,1)} %collective-permute-done.2.tiles_other, ...), custom_call_target="tpu_custom_call" | custom-call | flops 268435456 | bytes 8388608 | tf_op jit(solution)/shard_map/grad_sums/pallas_call | solution.py:438
  199.6 5.9 %grad_sums.7 = (bf16[2,128,1536]{2,1,0:T(8,128)(2,1)S(1)}, bf16[2,128,1536]{2,1,0:T(8,128)(2,1)}) custom-call(s32[23]{0:T(128)S(1)} %fusion.12.ids, s32[298]{0:T(512)S(1)} %pad_add_fusion.1.meta_own, s32[298]{0:T(512)S(1)} %collective-permute-done.meta_other, bf16[72,128,128]{2,1,0:T(8,128)(2,1)} %tiles_own.9, ...), custom_call_target="tpu_custom_call" | custom-call | flops 268435456 | bytes 8388608 | tf_op jit(solution)/shard_map/grad_sums/pallas_call | solution.py:438
  207.1 1.5 collective-permute-start.10
  208.6 1.6 tile_sums.23
  210.1 11.0 %collective-permute-start.7 = (bf16[2,48,3072]{2,1,0:T(8,128)(2,1)}, bf16[2,48,3072]{2,1,0:T(8,128)(2,1)}, u32[]{:S(2)}, u32[]{:S(2)}) collective-permute-start(bf16[2,48,3072]{2,1,0:T(8,128)(2,1)} %tile_sums.23), channel_id=1, source_target_pairs={{0,8},{2,10},{4,12},{6,14},{1,9},{3,11},{5,13},{7,15}} | collective-permute-start | bytes 1769480 | tf_op jit(solution)/shard_map/ppermute | solution.py:515
  221.1 2.0 tile_sums.35
  224.4 3.4 tile_sums.32
  228.6 6.3 %collective-permute-start.15 = (bf16[2,2,80,3072]{3,2,1,0:T(8,128)(2,1)}, bf16[2,2,80,3072]{3,2,1,0:T(8,128)(2,1)}, u32[]{:S(2)}, u32[]{:S(2)}) collective-permute-start(bf16[2,2,80,3072]{3,2,1,0:T(8,128)(2,1)} %tile_sums.32), channel_id=1, source_target_pairs={{0,8},{2,10},{4,12},{6,14},{8,16},{10,18},{12,20},{14,22},{16,24},... | collective-permute-start | bytes 5898248 | tf_op jit(solution)/shard_map/ppermute | solution.py:515
  234.9 2.3 copy-done.2
  238.3 2.1 tile_sums.27
  240.4 1.6 collective-permute-start.11
  242.0 2.5 tile_sums.24
  244.5 2.1 collective-permute-start.8
  249.2 4.6 %all-to-all-start.1 = ((bf16[2,256,1536]{2,1,0:T(8,128)(2,1)}), bf16[2,256,1536]{2,1,0:T(8,128)(2,1)}, u32[]{:S(2)}, u32[]{:S(2)}) async-start(bf16[2,256,1536]{2,1,0:T(8,128)(2,1)} %pad_maximum_fusion.2), calls=%async_computation.1 | async-start | bytes 3145728 | tf_op jit(solution)/shard_map/all_to_all | solution.py:608
  253.8 2.3 copy-done.3
  259.8 28.9 %collective-permute-done.8.refs_1_ = bf16[2,48,3072]{2,1,0:T(8,128)(2,1)} collective-permute-done((bf16[2,48,3072]{2,1,0:T(8,128)(2,1)}, bf16[2,48,3072]{2,1,0:T(8,128)(2,1)}, u32[]{:S(2)}, u32[]{:S(2)}) %collective-permute-start.8) | collective-permute-done | bytes 589856 | tf_op jit(solution)/shard_map/ppermute | solution.py:515
  288.7 1.5 tile_sums.25
  290.2 4.6 %collective-permute-start.9 = (bf16[2,48,3072]{2,1,0:T(8,128)(2,1)S(1)}, bf16[2,48,3072]{2,1,0:T(8,128)(2,1)S(1)}, u32[]{:S(2)}, u32[]{:S(2)}) collective-permute-start(bf16[2,48,3072]{2,1,0:T(8,128)(2,1)S(1)} %tile_sums.25), channel_id=1, source_target_pairs={{0,8},{2,10},{4,12},{6,14},{8,16},{10,18},{12,20},{14,22},{16,24},... | collective-permute-start | bytes 1769480 | tf_op jit(solution)/shard_map/ppermute | solution.py:515
  294.8 4.2 %collective-permute-done.12.refs_2_ = bf16[2,48,3072]{2,1,0:T(8,128)(2,1)S(1)} collective-permute-done((bf16[2,48,3072]{2,1,0:T(8,128)(2,1)S(1)}, bf16[2,48,3072]{2,1,0:T(8,128)(2,1)S(1)}, u32[]{:S(2)}, u32[]{:S(2)}) %collective-permute-start.12) | collective-permute-done | bytes 589856 | tf_op jit(solution)/shard_map/ppermute | solution.py:515
  299.0 7.6 %collective-permute-done.9.refs_1_ = bf16[2,48,3072]{2,1,0:T(8,128)(2,1)S(1)} collective-permute-done((bf16[2,48,3072]{2,1,0:T(8,128)(2,1)S(1)}, bf16[2,48,3072]{2,1,0:T(8,128)(2,1)S(1)}, u32[]{:S(2)}, u32[]{:S(2)}) %collective-permute-start.9) | collective-permute-done | bytes 589856 | tf_op jit(solution)/shard_map/ppermute | solution.py:515
  306.6 1.7 tile_sums.29
  309.1 3.2 tile_sums.36
  312.2 3.0 fusion.7
  315.3 1.8 convolution_convert_fusion.1
  317.1 4.9 %all-to-all-start.2 = ((bf16[32,16,512]{2,1,0:T(8,128)(2,1)}), bf16[32,16,512]{2,1,0:T(8,128)(2,1)}, u32[]{:S(2)}, u32[]{:S(2)}) async-start(bf16[32,16,512]{2,1,0:T(8,128)(2,1)} %bitcast.37), calls=%async_computation.2 | async-start | bytes 1048576 | tf_op jit(solution)/shard_map/all_to_all | solution.py:619
  322.0 1.7 constant_dynamic-update-slice_fusion.1
  323.7 1.7 constant_dynamic-update-slice_fusion.3
  325.4 16.0 %collective-permute-done.19.refs_2_ = bf16[2,80,3072]{2,1,0:T(8,128)(2,1)} collective-permute-done((bf16[2,80,3072]{2,1,0:T(8,128)(2,1)}, bf16[2,80,3072]{2,1,0:T(8,128)(2,1)}, u32[]{:S(2)}, u32[]{:S(2)}) %collective-permute-start.19) | collective-permute-done | bytes 983072 | tf_op jit(solution)/shard_map/ppermute | solution.py:515
  341.4 2.3 copy-done.4
  343.7 3.5 tile_sums.37
  347.2 2.2 convolution_convert_fusion
  352.2 3.5 all-to-all-start.3
  358.3 12.4 %all-to-all-done.3 = bf16[32,16,512]{2,1,0:T(8,128)(2,1)S(1)} async-done(((bf16[32,16,512]{2,1,0:T(8,128)(2,1)}), bf16[32,16,512]{2,1,0:T(8,128)(2,1)S(1)}, u32[]{:S(2)}, u32[]{:S(2)}) %all-to-all-start.3) | async-done | bytes 524320 | tf_op jit(solution)/shard_map/all_to_all | solution.py:623
  (148 shorter events, 38.8 us)
Async XLA Ops:
  0.6 5.1 %copy-start = (bf16[1536,512]{1,0:T(8,128)(2,1)S(1)}, bf16[1536,512]{1,0:T(8,128)(2,1)}, u32[]{:S(2)}) copy-start(bf16[1536,512]{1,0:T(8,128)(2,1)} %param.10) | copy-start | bytes 4718596
  0.6 3.1 copy-start.37
  0.7 3.0 copy-start.36
  3.2 2.6 copy-start.31
  3.2 10.3 %collective-permute-start.22 = (bf16[128,3072]{1,0:T(8,128)(2,1)S(1)}, bf16[128,3072]{1,0:T(8,128)(2,1)S(1)}, u32[]{:S(2)}, u32[]{:S(2)}) collective-permute-start(bf16[128,3072]{1,0:T(8,128)(2,1)S(1)} %get-tuple-element.18), channel_id=1, source_target_pairs={{0,2},{2,0},{4,6},{6,4},{8,10},{10,8},{12,14},{14,12},{16,18},{18,... | collective-permute-start | bytes 2359304 | tf_op jit(solution)/shard_map/ppermute | solution.py:515
  3.7 60.4 %collective-permute-start.2 = (bf16[72,128,128]{2,1,0:T(8,128)(2,1)}, bf16[72,128,128]{2,1,0:T(8,128)(2,1)}, u32[]{:S(2)}, u32[]{:S(2)}) collective-permute-start(bf16[72,128,128]{2,1,0:T(8,128)(2,1)} %tiles_own.9), channel_id=1, source_target_pairs={{0,2},{2,0},{4,6},{6,4},{8,10},{10,8},{12,14},{14,12},{16,18},{18,... | collective-permute-start | bytes 7077896 | tf_op jit(solution)/shard_map/ppermute | solution.py:515
  8.7 4.7 %copy-start.33 = (s32[72,1]{0,1:T(1,128)S(1)}, s32[72,1]{0,1:T(1,128)}, u32[]{:S(2)}) copy-start(s32[72,1]{0,1:T(1,128)} %param.15) | copy-start | bytes 868
  8.7 25.8 %all-to-all-start = ((bf16[2,256,1536]{2,1,0:T(8,128)(2,1)}), bf16[2,256,1536]{2,1,0:T(8,128)(2,1)}, u32[]{:S(2)}, u32[]{:S(2)}) async-start(bf16[2,256,1536]{2,1,0:T(8,128)(2,1)} %bitcast.7), calls=%async_computation | async-start | bytes 3145728 | tf_op jit(solution)/shard_map/all_to_all | solution.py:553
  13.4 9.9 %copy-start.34 = (s32[72]{0:T(128)S(1)}, s32[72]{0:T(128)}, u32[]{:S(2)}) copy-start(s32[72]{0:T(128)} %param.17) | copy-start | bytes 868
  13.5 9.9 %copy-start.35 = (s32[72]{0:T(128)S(1)}, s32[72]{0:T(128)}, u32[]{:S(2)}) copy-start(s32[72]{0:T(128)} %param.16) | copy-start | bytes 868
  15.9 38.8 %collective-permute-start.23 = (bf16[2,128,3072]{2,1,0:T(8,128)(2,1)S(1)}, bf16[2,128,3072]{2,1,0:T(8,128)(2,1)}, u32[]{:S(2)}, u32[]{:S(2)}) collective-permute-start(bf16[2,128,3072]{2,1,0:T(8,128)(2,1)S(1)} %pad_maximum_fusion.1.refs_0_), channel_id=1, source_target_pairs={{0,8},{2,10},{4,12},{6,14},{8,16},{10,18},{12,20},{14,22},{16,24},... | collective-permute-start | bytes 4718600 | tf_op jit(solution)/shard_map/ppermute | solution.py:515
  22.1 38.0 %collective-permute-start.26 = (bf16[2,128,3072]{2,1,0:T(8,128)(2,1)S(1)}, bf16[2,128,3072]{2,1,0:T(8,128)(2,1)}, u32[]{:S(2)}, u32[]{:S(2)}) collective-permute-start(bf16[2,128,3072]{2,1,0:T(8,128)(2,1)S(1)} %pad_maximum_fusion.1.refs_0_), channel_id=1, source_target_pairs={{8,0},{10,2},{12,4},{14,6},{16,8},{18,10},{20,12},{22,14},{24,16},... | collective-permute-start | bytes 4718600 | tf_op jit(solution)/shard_map/ppermute | solution.py:515
  24.1 12.7 %collective-permute-start = (s32[298]{0:T(512)S(1)}, s32[298]{0:T(512)S(1)}, u32[]{:S(2)}, u32[]{:S(2)}) collective-permute-start(s32[298]{0:T(512)S(1)} %pad_add_fusion.1.meta_own), channel_id=1, source_target_pairs={{0,2},{2,0},{4,6},{6,4},{8,10},{10,8},{12,14},{14,12},{16,18},{18,... | collective-permute-start | bytes 3584 | tf_op jit(solution)/shard_map/ppermute | solution.py:515
  24.1 57.1 %collective-permute-start.35 = (bf16[2,128,3072]{2,1,0:T(8,128)(2,1)S(1)}, bf16[2,128,3072]{2,1,0:T(8,128)(2,1)}, u32[]{:S(2)}, u32[]{:S(2)}) collective-permute-start(bf16[2,128,3072]{2,1,0:T(8,128)(2,1)S(1)} %pad_maximum_fusion.1.refs_0_), channel_id=1, source_target_pairs={{0,4},{2,6},{4,0},{6,2},{8,12},{10,14},{12,8},{14,10},{16,20},{18,... | collective-permute-start | bytes 4718600 | tf_op jit(solution)/shard_map/ppermute | solution.py:515
  36.8 24.6 %collective-permute-start.1 = (bf16[2,128,1536]{2,1,0:T(8,128)(2,1)S(1)}, bf16[2,128,1536]{2,1,0:T(8,128)(2,1)S(1)}, u32[]{:S(2)}, u32[]{:S(2)}) collective-permute-start(bf16[2,128,1536]{2,1,0:T(8,128)(2,1)S(1)} %get-tuple-element.21), channel_id=1, source_target_pairs={{0,2},{2,0},{4,6},{6,4},{8,10},{10,8},{12,14},{14,12},{16,18},{18,... | collective-permute-start | bytes 2359304 | tf_op jit(solution)/shard_map/ppermute | solution.py:515
  54.7 28.3 %collective-permute-start.24 = (bf16[2,128,3072]{2,1,0:T(8,128)(2,1)}, bf16[2,128,3072]{2,1,0:T(8,128)(2,1)}, u32[]{:S(2)}, u32[]{:S(2)}) collective-permute-start(bf16[2,128,3072]{2,1,0:T(8,128)(2,1)} %collective-permute-done.23.refs_1_), channel_id=1, source_target_pairs={{8,16},{10,18},{12,20},{14,22},{16,24},{18,26},{20,28},{22,30},{9,... | collective-permute-start | bytes 4718600 | tf_op jit(solution)/shard_map/ppermute | solution.py:515
  60.1 37.5 %collective-permute-start.27 = (bf16[2,128,3072]{2,1,0:T(8,128)(2,1)}, bf16[2,128,3072]{2,1,0:T(8,128)(2,1)}, u32[]{:S(2)}, u32[]{:S(2)}) collective-permute-start(bf16[2,128,3072]{2,1,0:T(8,128)(2,1)} %collective-permute-done.26.refs_2_), channel_id=1, source_target_pairs={{8,0},{10,2},{12,4},{14,6},{16,8},{18,10},{20,12},{22,14},{9,1},{1... | collective-permute-start | bytes 4718600 | tf_op jit(solution)/shard_map/ppermute | solution.py:515
  62.3 36.1 %collective-permute-start.33 = (bf16[2,128,3072]{2,1,0:T(8,128)(2,1)}, bf16[2,128,3072]{2,1,0:T(8,128)(2,1)}, u32[]{:S(2)}, u32[]{:S(2)}) collective-permute-start(bf16[2,128,3072]{2,1,0:T(8,128)(2,1)} %collective-permute-done.23.refs_1_), channel_id=1, source_target_pairs={{8,12},{10,14},{12,8},{14,10},{16,20},{18,22},{20,16},{22,18},{24,... | collective-permute-start | bytes 4718600 | tf_op jit(solution)/shard_map/ppermute | solution.py:515
  64.1 37.4 %collective-permute-start.34 = (bf16[2,128,3072]{2,1,0:T(8,128)(2,1)}, bf16[2,128,3072]{2,1,0:T(8,128)(2,1)}, u32[]{:S(2)}, u32[]{:S(2)}) collective-permute-start(bf16[2,128,3072]{2,1,0:T(8,128)(2,1)} %collective-permute-done.26.refs_2_), channel_id=1, source_target_pairs={{0,4},{2,6},{4,0},{6,2},{8,12},{10,14},{12,8},{14,10},{16,20},{18,... | collective-permute-start | bytes 4718600 | tf_op jit(solution)/shard_map/ppermute | solution.py:515
  80.4 144.0 %copy-start.1 = (bf16[2,72,128,128]{3,2,1,0:T(8,128)(2,1)}, bf16[2,72,128,128]{3,2,1,0:T(8,128)(2,1)S(1)}, u32[]{:S(2)}) copy-start(bf16[2,72,128,128]{3,2,1,0:T(8,128)(2,1)S(1)} %tile_parts.1.parts) | copy-start | bytes 14155780
  81.2 21.0 %collective-permute-start.16 = (bf16[2,2,80,3072]{3,2,1,0:T(8,128)(2,1)S(1)}, bf16[2,2,80,3072]{3,2,1,0:T(8,128)(2,1)S(1)}, u32[]{:S(2)}, u32[]{:S(2)}) collective-permute-start(bf16[2,2,80,3072]{3,2,1,0:T(8,128)(2,1)S(1)} %tile_sums.33), channel_id=1, source_target_pairs={{24,16},{26,18},{28,20},{30,22},{25,17},{27,19},{29,21},{31,23}} | collective-permute-start | bytes 5898248 | tf_op jit(solution)/shard_map/ppermute | solution.py:515
  83.1 53.4 %collective-permute-start.13 = (bf16[2,2,80,3072]{3,2,1,0:T(8,128)(2,1)S(1)}, bf16[2,2,80,3072]{3,2,1,0:T(8,128)(2,1)S(1)}, u32[]{:S(2)}, u32[]{:S(2)}) collective-permute-start(bf16[2,2,80,3072]{3,2,1,0:T(8,128)(2,1)S(1)} %tile_sums.30), channel_id=1, source_target_pairs={{0,8},{2,10},{4,12},{6,14},{1,9},{3,11},{5,13},{7,15}} | collective-permute-start | bytes 5898248 | tf_op jit(solution)/shard_map/ppermute | solution.py:515
  97.6 8.0 %collective-permute-start.29 = (bf16[2,128,3072]{2,1,0:T(8,128)(2,1)}, bf16[2,128,3072]{2,1,0:T(8,128)(2,1)S(1)}, u32[]{:S(2)}, u32[]{:S(2)}) collective-permute-start(bf16[2,128,3072]{2,1,0:T(8,128)(2,1)} %collective-permute-done.24.refs_1_), channel_id=1, source_target_pairs={{16,24},{18,26},{20,28},{22,30},{17,25},{19,27},{21,29},{23,31}} | collective-permute-start | bytes 4718600 | tf_op jit(solution)/shard_map/ppermute | solution.py:515
  98.3 38.9 %collective-permute-start.31 = (bf16[2,128,3072]{2,1,0:T(8,128)(2,1)}, bf16[2,128,3072]{2,1,0:T(8,128)(2,1)S(1)}, u32[]{:S(2)}, u32[]{:S(2)}) collective-permute-start(bf16[2,128,3072]{2,1,0:T(8,128)(2,1)} %collective-permute-done.27.refs_2_), channel_id=1, source_target_pairs={{8,0},{10,2},{12,4},{14,6},{9,1},{11,3},{13,5},{15,7}} | collective-permute-start | bytes 4718600 | tf_op jit(solution)/shard_map/ppermute | solution.py:515
  101.4 42.1 %collective-permute-start.25 = (bf16[2,128,3072]{2,1,0:T(8,128)(2,1)}, bf16[2,128,3072]{2,1,0:T(8,128)(2,1)S(1)}, u32[]{:S(2)}, u32[]{:S(2)}) collective-permute-start(bf16[2,128,3072]{2,1,0:T(8,128)(2,1)} %collective-permute-done.24.refs_1_), channel_id=1, source_target_pairs={{16,20},{18,22},{20,16},{22,18},{24,28},{26,30},{28,24},{30,26},{1... | collective-permute-start | bytes 4718600 | tf_op jit(solution)/shard_map/ppermute | solution.py:515
  102.2 48.7 %collective-permute-start.28 = (bf16[2,128,3072]{2,1,0:T(8,128)(2,1)}, bf16[2,128,3072]{2,1,0:T(8,128)(2,1)S(1)}, u32[]{:S(2)}, u32[]{:S(2)}) collective-permute-start(bf16[2,128,3072]{2,1,0:T(8,128)(2,1)} %collective-permute-done.27.refs_2_), channel_id=1, source_target_pairs={{0,4},{2,6},{4,0},{6,2},{8,12},{10,14},{12,8},{14,10},{1,5},{3,7},... | collective-permute-start | bytes 4718600 | tf_op jit(solution)/shard_map/ppermute | solution.py:515
  105.6 47.6 %collective-permute-start.30 = (bf16[2,128,3072]{2,1,0:T(8,128)(2,1)S(1)}, bf16[2,128,3072]{2,1,0:T(8,128)(2,1)S(1)}, u32[]{:S(2)}, u32[]{:S(2)}) collective-permute-start(bf16[2,128,3072]{2,1,0:T(8,128)(2,1)S(1)} %collective-permute-done.29.refs_2_), channel_id=1, source_target_pairs={{24,28},{26,30},{28,24},{30,26},{25,29},{27,31},{29,25},{31,27}} | collective-permute-start | bytes 4718600 | tf_op jit(solution)/shard_map/ppermute | solution.py:515
  136.5 73.7 %collective-permute-start.17 = (bf16[2,2,80,3072]{3,2,1,0:T(8,128)(2,1)S(1)}, bf16[2,2,80,3072]{3,2,1,0:T(8,128)(2,1)S(1)}, u32[]{:S(2)}, u32[]{:S(2)}) collective-permute-start(bf16[2,2,80,3072]{3,2,1,0:T(8,128)(2,1)S(1)} %tile_sums.34), channel_id=1, source_target_pairs={{16,8},{18,10},{20,12},{22,14},{24,16},{26,18},{28,20},{30,22},{17... | collective-permute-start | bytes 5898248 | tf_op jit(solution)/shard_map/ppermute | solution.py:515
  137.3 6.3 %copy-start.12 = (bf16[2,128,3072]{2,1,0:T(8,128)(2,1)}, bf16[2,128,3072]{2,1,0:T(8,128)(2,1)S(1)}, u32[]{:S(2)}) copy-start(bf16[2,128,3072]{2,1,0:T(8,128)(2,1)S(1)} %collective-permute-done.31.refs_3_) | copy-start | bytes 4718596
  137.3 39.2 %collective-permute-start.32 = (bf16[2,128,3072]{2,1,0:T(8,128)(2,1)S(1)}, bf16[2,128,3072]{2,1,0:T(8,128)(2,1)S(1)}, u32[]{:S(2)}, u32[]{:S(2)}) collective-permute-start(bf16[2,128,3072]{2,1,0:T(8,128)(2,1)S(1)} %collective-permute-done.31.refs_3_), channel_id=1, source_target_pairs={{0,4},{2,6},{4,0},{6,2},{1,5},{3,7},{5,1},{7,3}} | collective-permute-start | bytes 4718600 | tf_op jit(solution)/shard_map/ppermute | solution.py:515
  143.5 7.4 %copy-start.14 = (bf16[2,128,3072]{2,1,0:T(8,128)(2,1)}, bf16[2,128,3072]{2,1,0:T(8,128)(2,1)S(1)}, u32[]{:S(2)}) copy-start(bf16[2,128,3072]{2,1,0:T(8,128)(2,1)S(1)} %collective-permute-done.25.refs_0_) | copy-start | bytes 4718596
  143.5 79.6 %collective-permute-start.14 = (bf16[2,2,80,3072]{3,2,1,0:T(8,128)(2,1)}, bf16[2,2,80,3072]{3,2,1,0:T(8,128)(2,1)}, u32[]{:S(2)}, u32[]{:S(2)}) collective-permute-start(bf16[2,2,80,3072]{3,2,1,0:T(8,128)(2,1)} %tile_sums.31), channel_id=1, source_target_pairs={{0,8},{2,10},{4,12},{6,14},{8,16},{10,18},{12,20},{14,22},{1,9},{3... | collective-permute-start | bytes 5898248 | tf_op jit(solution)/shard_map/ppermute | solution.py:515
  150.9 54.6 %collective-permute-start.4 = (bf16[2,48,3072]{2,1,0:T(8,128)(2,1)}, bf16[2,48,3072]{2,1,0:T(8,128)(2,1)S(1)}, u32[]{:S(2)}, u32[]{:S(2)}) collective-permute-start(bf16[2,48,3072]{2,1,0:T(8,128)(2,1)} %tile_sums.20), channel_id=1, source_target_pairs={{0,4},{2,6},{4,0},{6,2},{8,12},{10,14},{12,8},{14,10},{16,20},{18,... | collective-permute-start | bytes 1769480 | tf_op jit(solution)/shard_map/ppermute | solution.py:515
  153.2 3.3 copy-start.18
  153.2 53.8 %collective-permute-start.6 = (bf16[2,48,3072]{2,1,0:T(8,128)(2,1)}, bf16[2,48,3072]{2,1,0:T(8,128)(2,1)S(1)}, u32[]{:S(2)}, u32[]{:S(2)}) collective-permute-start(bf16[2,48,3072]{2,1,0:T(8,128)(2,1)} %tile_sums.22), channel_id=1, source_target_pairs={{0,4},{2,6},{4,0},{6,2},{8,12},{10,14},{12,8},{14,10},{16,20},{18,... | collective-permute-start | bytes 1769480 | tf_op jit(solution)/shard_map/ppermute | solution.py:515
  177.6 50.2 %collective-permute-start.5 = (bf16[2,48,3072]{2,1,0:T(8,128)(2,1)}, bf16[2,48,3072]{2,1,0:T(8,128)(2,1)S(1)}, u32[]{:S(2)}, u32[]{:S(2)}) collective-permute-start(bf16[2,48,3072]{2,1,0:T(8,128)(2,1)} %tile_sums.21), channel_id=1, source_target_pairs={{0,4},{2,6},{4,0},{6,2},{8,12},{10,14},{12,8},{14,10},{16,20},{18,... | collective-permute-start | bytes 1769480 | tf_op jit(solution)/shard_map/ppermute | solution.py:515
  184.5 6.9 %copy-start.13 = (bf16[2,128,3072]{2,1,0:T(8,128)(2,1)S(1)}, bf16[2,128,3072]{2,1,0:T(8,128)(2,1)}, u32[]{:S(2)}) copy-start(bf16[2,128,3072]{2,1,0:T(8,128)(2,1)} %copy-done.12) | copy-start | bytes 4718596
  191.4 5.4 %copy-start.15 = (bf16[2,128,3072]{2,1,0:T(8,128)(2,1)S(1)}, bf16[2,128,3072]{2,1,0:T(8,128)(2,1)}, u32[]{:S(2)}) copy-start(bf16[2,128,3072]{2,1,0:T(8,128)(2,1)} %copy-done.14) | copy-start | bytes 4718596
  191.4 5.4 %copy-start.19 = (bf16[2,128,3072]{2,1,0:T(8,128)(2,1)S(1)}, bf16[2,128,3072]{2,1,0:T(8,128)(2,1)}, u32[]{:S(2)}) copy-start(bf16[2,128,3072]{2,1,0:T(8,128)(2,1)} %copy-done.18) | copy-start | bytes 4718596
  205.5 41.1 %collective-permute-start.36 = (bf16[2,128,1536]{2,1,0:T(8,128)(2,1)}, bf16[2,128,1536]{2,1,0:T(8,128)(2,1)}, u32[]{:S(2)}, u32[]{:S(2)}) collective-permute-start(bf16[2,128,1536]{2,1,0:T(8,128)(2,1)} %get-tuple-element.14), channel_id=1, source_target_pairs={{0,2},{2,0},{4,6},{6,4},{8,10},{10,8},{12,14},{14,12},{16,18},{18,... | collective-permute-start | bytes 2359304 | tf_op jit(solution)/shard_map/ppermute | solution.py:515
  207.1 3.1 copy-start.10
  207.1 27.8 %collective-permute-start.10 = (bf16[2,48,3072]{2,1,0:T(8,128)(2,1)}, bf16[2,48,3072]{2,1,0:T(8,128)(2,1)}, u32[]{:S(2)}, u32[]{:S(2)}) collective-permute-start(bf16[2,48,3072]{2,1,0:T(8,128)(2,1)} %tile_sums.26), channel_id=1, source_target_pairs={{24,16},{26,18},{28,20},{30,22},{25,17},{27,19},{29,21},{31,23}} | collective-permute-start | bytes 1769480 | tf_op jit(solution)/shard_map/ppermute | solution.py:515
  210.1 31.9 %collective-permute-start.7 = (bf16[2,48,3072]{2,1,0:T(8,128)(2,1)}, bf16[2,48,3072]{2,1,0:T(8,128)(2,1)}, u32[]{:S(2)}, u32[]{:S(2)}) collective-permute-start(bf16[2,48,3072]{2,1,0:T(8,128)(2,1)} %tile_sums.23), channel_id=1, source_target_pairs={{0,8},{2,10},{4,12},{6,14},{1,9},{3,11},{5,13},{7,15}} | collective-permute-start | bytes 1769480 | tf_op jit(solution)/shard_map/ppermute | solution.py:515
  223.1 86.0 %collective-permute-start.18 = (bf16[2,2,80,3072]{3,2,1,0:T(8,128)(2,1)}, bf16[2,2,80,3072]{3,2,1,0:T(8,128)(2,1)S(1)}, u32[]{:S(2)}, u32[]{:S(2)}) collective-permute-start(bf16[2,2,80,3072]{3,2,1,0:T(8,128)(2,1)} %tile_sums.35), channel_id=1, source_target_pairs={{8,0},{10,2},{12,4},{14,6},{16,8},{18,10},{20,12},{22,14},{24,16},... | collective-permute-start | bytes 5898248 | tf_op jit(solution)/shard_map/ppermute | solution.py:515
  228.6 80.4 %collective-permute-start.15 = (bf16[2,2,80,3072]{3,2,1,0:T(8,128)(2,1)}, bf16[2,2,80,3072]{3,2,1,0:T(8,128)(2,1)}, u32[]{:S(2)}, u32[]{:S(2)}) collective-permute-start(bf16[2,2,80,3072]{3,2,1,0:T(8,128)(2,1)} %tile_sums.32), channel_id=1, source_target_pairs={{0,8},{2,10},{4,12},{6,14},{8,16},{10,18},{12,20},{14,22},{16,24},... | collective-permute-start | bytes 5898248 | tf_op jit(solution)/shard_map/ppermute | solution.py:515
  234.9 2.3 copy-start.2
  240.4 6.2 %copy-start.25 = (bf16[2,128,1536]{2,1,0:T(8,128)(2,1)S(1)}, bf16[2,128,1536]{2,1,0:T(8,128)(2,1)}, u32[]{:S(2)}) copy-start(bf16[2,128,1536]{2,1,0:T(8,128)(2,1)} %copy-done.24) | copy-start | bytes 2359300
  240.4 16.8 %collective-permute-start.11 = (bf16[2,48,3072]{2,1,0:T(8,128)(2,1)}, bf16[2,48,3072]{2,1,0:T(8,128)(2,1)}, u32[]{:S(2)}, u32[]{:S(2)}) collective-permute-start(bf16[2,48,3072]{2,1,0:T(8,128)(2,1)} %tile_sums.27), channel_id=1, source_target_pairs={{16,8},{18,10},{20,12},{22,14},{24,16},{26,18},{28,20},{30,22},{17... | collective-permute-start | bytes 1769480 | tf_op jit(solution)/shard_map/ppermute | solution.py:515
  244.5 44.2 %collective-permute-start.8 = (bf16[2,48,3072]{2,1,0:T(8,128)(2,1)}, bf16[2,48,3072]{2,1,0:T(8,128)(2,1)}, u32[]{:S(2)}, u32[]{:S(2)}) collective-permute-start(bf16[2,48,3072]{2,1,0:T(8,128)(2,1)} %tile_sums.24), channel_id=1, source_target_pairs={{0,8},{2,10},{4,12},{6,14},{8,16},{10,18},{12,20},{14,22},{1,9},{3... | collective-permute-start | bytes 1769480 | tf_op jit(solution)/shard_map/ppermute | solution.py:515
  249.2 63.0 %all-to-all-start.1 = ((bf16[2,256,1536]{2,1,0:T(8,128)(2,1)}), bf16[2,256,1536]{2,1,0:T(8,128)(2,1)}, u32[]{:S(2)}, u32[]{:S(2)}) async-start(bf16[2,256,1536]{2,1,0:T(8,128)(2,1)} %pad_maximum_fusion.2), calls=%async_computation.1 | async-start | bytes 3145728 | tf_op jit(solution)/shard_map/all_to_all | solution.py:608
  253.8 2.3 copy-start.3
  257.1 31.6 %copy-start.9 = (bf16[2,48,3072]{2,1,0:T(8,128)(2,1)S(1)}, bf16[2,48,3072]{2,1,0:T(8,128)(2,1)}, u32[]{:S(2)}) copy-start(bf16[2,48,3072]{2,1,0:T(8,128)(2,1)} %copy-done.8) | copy-start | bytes 1769476
  257.1 37.7 %collective-permute-start.3 = (bf16[2,48,3072]{2,1,0:T(8,128)(2,1)S(1)}, bf16[2,48,3072]{2,1,0:T(8,128)(2,1)S(1)}, u32[]{:S(2)}, u32[]{:S(2)}) collective-permute-start(bf16[2,48,3072]{2,1,0:T(8,128)(2,1)S(1)} %tile_sums.19), channel_id=1, source_target_pairs={{0,4},{2,6},{4,0},{6,2},{8,12},{10,14},{12,8},{14,10},{16,20},{18,... | collective-permute-start | bytes 1769480 | tf_op jit(solution)/shard_map/ppermute | solution.py:515
  258.5 40.5 %collective-permute-start.12 = (bf16[2,48,3072]{2,1,0:T(8,128)(2,1)S(1)}, bf16[2,48,3072]{2,1,0:T(8,128)(2,1)S(1)}, u32[]{:S(2)}, u32[]{:S(2)}) collective-permute-start(bf16[2,48,3072]{2,1,0:T(8,128)(2,1)S(1)} %tile_sums.28), channel_id=1, source_target_pairs={{8,0},{10,2},{12,4},{14,6},{16,8},{18,10},{20,12},{22,14},{24,16},... | collective-permute-start | bytes 1769480 | tf_op jit(solution)/shard_map/ppermute | solution.py:515
  290.2 16.4 %collective-permute-start.9 = (bf16[2,48,3072]{2,1,0:T(8,128)(2,1)S(1)}, bf16[2,48,3072]{2,1,0:T(8,128)(2,1)S(1)}, u32[]{:S(2)}, u32[]{:S(2)}) collective-permute-start(bf16[2,48,3072]{2,1,0:T(8,128)(2,1)S(1)} %tile_sums.25), channel_id=1, source_target_pairs={{0,8},{2,10},{4,12},{6,14},{8,16},{10,18},{12,20},{14,22},{16,24},... | collective-permute-start | bytes 1769480 | tf_op jit(solution)/shard_map/ppermute | solution.py:515
  309.1 14.7 %collective-permute-start.20 = (bf16[48,3072]{1,0:T(8,128)(2,1)}, bf16[48,3072]{1,0:T(8,128)(2,1)}, u32[]{:S(2)}, u32[]{:S(2)}) collective-permute-start(bf16[48,3072]{1,0:T(8,128)(2,1)} %get-tuple-element.11), channel_id=1, source_target_pairs={{0,2},{2,0},{4,6},{6,4},{8,10},{10,8},{12,14},{14,12},{16,18},{18,... | collective-permute-start | bytes 884744 | tf_op jit(solution)/shard_map/ppermute | solution.py:515
  312.2 29.2 %collective-permute-start.19 = (bf16[2,80,3072]{2,1,0:T(8,128)(2,1)}, bf16[2,80,3072]{2,1,0:T(8,128)(2,1)}, u32[]{:S(2)}, u32[]{:S(2)}) collective-permute-start(bf16[2,80,3072]{2,1,0:T(8,128)(2,1)} %tile_sums.36), channel_id=1, source_target_pairs={{0,4},{2,6},{4,0},{6,2},{8,12},{10,14},{12,8},{14,10},{16,20},{18,... | collective-permute-start | bytes 2949128 | tf_op jit(solution)/shard_map/ppermute | solution.py:515
  317.1 33.1 %all-to-all-start.2 = ((bf16[32,16,512]{2,1,0:T(8,128)(2,1)}), bf16[32,16,512]{2,1,0:T(8,128)(2,1)}, u32[]{:S(2)}, u32[]{:S(2)}) async-start(bf16[32,16,512]{2,1,0:T(8,128)(2,1)} %bitcast.37), calls=%async_computation.2 | async-start | bytes 1048576 | tf_op jit(solution)/shard_map/all_to_all | solution.py:619
  341.4 2.3 copy-start.4
  343.7 3.5 copy-start.28
  343.7 3.5 copy-start.32
  347.2 8.5 %collective-permute-start.21 = (bf16[80,3072]{1,0:T(8,128)(2,1)}, bf16[80,3072]{1,0:T(8,128)(2,1)S(1)}, u32[]{:S(2)}, u32[]{:S(2)}) collective-permute-start(bf16[80,3072]{1,0:T(8,128)(2,1)} %get-tuple-element.12), channel_id=1, source_target_pairs={{0,2},{2,0},{4,6},{6,4},{8,10},{10,8},{12,14},{14,12},{16,18},{18,... | collective-permute-start | bytes 1474568 | tf_op jit(solution)/shard_map/ppermute | solution.py:515
  349.4 6.3 %copy-start.29 = (bf16[128,3072]{1,0:T(8,128)(2,1)S(1)}, bf16[128,3072]{1,0:T(8,128)(2,1)}, u32[]{:S(2)}) copy-start(bf16[128,3072]{1,0:T(8,128)(2,1)} %constant_dynamic-update-slice_fusion.3) | copy-start | bytes 2359300
  352.2 18.5 %all-to-all-start.3 = ((bf16[32,16,512]{2,1,0:T(8,128)(2,1)}), bf16[32,16,512]{2,1,0:T(8,128)(2,1)S(1)}, u32[]{:S(2)}, u32[]{:S(2)}) async-start(bf16[32,16,512]{2,1,0:T(8,128)(2,1)} %broadcast_in_dim.2), calls=%async_computation.3 | async-start | bytes 1048576 | tf_op jit(solution)/shard_map/all_to_all | solution.py:623
  (15 other events, 19.0 us)

commit v2 on v1

--- a/solution.py
+++ b/solution.py
@@ -12,9 +12,9 @@
 F32 = jnp.float32
 BF16 = jnp.bfloat16
 VMEM_LIMIT = 48 * 1024 * 1024
-GRID_VMEM = 32 * 1024 * 1024
-PARTS_VMEM = 20 * 1024 * 1024
-SMALL_VMEM = 16 * 1024 * 1024
+GRID_VMEM = 24 * 1024 * 1024
+PARTS_VMEM = 16 * 1024 * 1024
+SMALL_VMEM = 10 * 1024 * 1024
 
 
 def gelu_value(v):
@@ -271,6 +271,7 @@
 
 
 GROUP = 4
+PARTS_GROUP = 8
 
 
 def each_tile(meta, base, chip, product, add):
@@ -305,12 +306,12 @@
             )
 
         def step(g, carry, q=q, product=product):
-            at = [g * GROUP + u for u in range(GROUP)]
+            at = [g * PARTS_GROUP + u for u in range(PARTS_GROUP)]
             for i, part in zip(at, [product(i) for i in at]):
                 out_ref[q, i] = part.astype(BF16)
             return carry
 
-        lax.fori_loop(0, count // GROUP, step, 0)
+        lax.fori_loop(0, count // PARTS_GROUP, step, 0)
 
 
 SMEM = pl.BlockSpec(memory_space=pltpu.SMEM)

time: 374 us -> 372 us (level)
  Pallas kernels: 69 us -> 63 us
    unnamed x79 -> x71, local copies, waits for them, and re-layouts: 22 us -> 21.4 us
  transfers between devices with their start and end apart: 41 -> 41, of which waited for: 12 -> 12; matrix products, arithmetic and copies ran while one was open for 8% -> 8% of each run, Pallas kernels for 19% -> 17%
where the time goes in v2:
time: 372 us; the launch traced here: 369 us
  waiting for transfers between devices  155 us (42%)
  starting transfers between devices  101 us (27%)
  Pallas kernels  63 us (17%)
  local copies, waits for them, and re-layouts  28.8 us (8%)
  other arithmetic  11.3 us (3%)
  matrix products  8.96 us (2%)
    ppermute x37, waiting for transfers between devices, permute(): return lax.ppermute(a, 'row', pairs)  134 us
    ppermute x37, starting transfers between devices, permute(): return lax.ppermute(a, 'row', pairs)  82.9 us
    pallas_call x19, Pallas kernels, tile_sums(): pl.pallas_call(functools.partial(sum_kernel, spec), out_shape=out, in_spe...  31.8 us
    pallas_call x4, Pallas kernels, grad_sums(): pl.pallas_call(functools.partial(grad_kernel, (tuple(chips), bool(sums),...  23.4 us
    unnamed x71, local copies, waits for them, and re-layouts  21.4 us
    all_to_all x1, waiting for transfers between devices, finish(): lax.all_to_all(jnp.broadcast_to(share[None], (devices,) + share.shape), a...  12.4 us
    all_to_all x1, waiting for transfers between devices, grid_device(): lax.all_to_all(msg_t.reshape(col_count, feats, nodes), 'col', split_axis=...  8.77 us
    pallas_call x1, Pallas kernels, tile_parts(): pl.pallas_call(parts_kernel, out_shape=jax.ShapeDtypeStruct((2, count, fe...  7.82 us
  transfers between devices with their start and end apart: 41, of which 12 were waited for; matrix products, arithmetic and copies ran while one was open for 8% of the time, Pallas kernels for 17%

profile of v2, /device:TPU:0, one launch (start us, length us, event | category | flops | bytes accessed | tf_op | source)
XLA Modules:
  0.0 369.5 jit_solution(5679188953797077885)
XLA Ops:
  0.7 2.5 dynamic-slice_bitcast_fusion
  3.7 2.1 fusion.1
  5.8 2.9 multiply_convert_fusion
  8.7 4.8 %all-to-all-start = ((bf16[2,256,1536]{2,1,0:T(8,128)(2,1)}), bf16[2,256,1536]{2,1,0:T(8,128)(2,1)}, u32[]{:S(2)}, u32[]{:S(2)}) async-start(bf16[2,256,1536]{2,1,0:T(8,128)(2,1)} %bitcast.7), calls=%async_computation | async-start | bytes 3145728 | tf_op jit(solution)/shard_map/all_to_all | solution.py:554
  14.4 1.5 pad_maximum_fusion.1.refs_0_
  16.0 6.1 %collective-permute-start.23 = (bf16[2,128,3072]{2,1,0:T(8,128)(2,1)S(1)}, bf16[2,128,3072]{2,1,0:T(8,128)(2,1)}, u32[]{:S(2)}, u32[]{:S(2)}) collective-permute-start(bf16[2,128,3072]{2,1,0:T(8,128)(2,1)S(1)} %pad_maximum_fusion.1.refs_0_), channel_id=1, source_target_pairs={{0,8},{2,10},{4,12},{6,14},{8,16},{10,18},{12,20},{14,22},{16,24},... | collective-permute-start | bytes 4718600 | tf_op jit(solution)/shard_map/ppermute | solution.py:516
  24.1 1.6 collective-permute-start.35
  25.7 8.8 %all-to-all-done = bf16[2,256,1536]{2,1,0:T(8,128)(2,1)} async-done(((bf16[2,256,1536]{2,1,0:T(8,128)(2,1)}), bf16[2,256,1536]{2,1,0:T(8,128)(2,1)}, u32[]{:S(2)}, u32[]{:S(2)}) %all-to-all-start) | async-done | bytes 1572896 | tf_op jit(solution)/shard_map/all_to_all | solution.py:554
  34.5 2.4 constant_dynamic-slice_fusion.1
  36.8 17.9 %collective-permute-done.23.refs_1_ = bf16[2,128,3072]{2,1,0:T(8,128)(2,1)} collective-permute-done((bf16[2,128,3072]{2,1,0:T(8,128)(2,1)S(1)}, bf16[2,128,3072]{2,1,0:T(8,128)(2,1)}, u32[]{:S(2)}, u32[]{:S(2)}) %collective-permute-start.23) | collective-permute-done | bytes 1572896 | tf_op jit(solution)/shard_map/ppermute | solution.py:516
  54.7 1.8 collective-permute-start.24
  56.5 3.6 collective-permute-done.26.refs_2_
  62.3 1.8 collective-permute-start.33
  64.1 3.4 collective-permute-start.34
  70.5 7.8 %tile_parts.1.parts = bf16[2,72,128,128]{3,2,1,0:T(8,128)(2,1)S(1)} custom-call(s32[298]{0:T(512)S(1)} %pad_add_fusion.1.meta_own, s32[298]{0:T(512)S(1)} %collective-permute-done.meta_other, bf16[2,128,1536]{2,1,0:T(8,128)(2,1)S(1)} %copy-done.5, bf16[2,128,1536]{2,1,0:T(8,128)(2,1)S(1)} %copy-done.19, bf16[72,128,128]{2,1,0:T(8,128)(2,1)} %tiles_own.9, ...), custom_call_target="tpu_custom_call" | custom-call | flops 1073741824 | bytes 12582912 | tf_op jit(solution)/shard_map/tile_parts/pallas_call | solution.py:324
  80.9 15.1 %collective-permute-start.13 = (bf16[2,2,80,3072]{3,2,1,0:T(8,128)(2,1)S(1)}, bf16[2,2,80,3072]{3,2,1,0:T(8,128)(2,1)S(1)}, u32[]{:S(2)}, u32[]{:S(2)}) collective-permute-start(bf16[2,2,80,3072]{3,2,1,0:T(8,128)(2,1)S(1)} %tile_sums.30), channel_id=1, source_target_pairs={{0,8},{2,10},{4,12},{6,14},{1,9},{3,11},{5,13},{7,15}} | collective-permute-start | bytes 5898248 | tf_op jit(solution)/shard_map/ppermute | solution.py:516
  96.1 1.5 collective-permute-done.27.refs_2_
  99.6 1.8 collective-permute-done.34.refs_1_
  102.2 3.4 collective-permute-start.28
  107.2 29.3 %collective-permute-done.13.refs_0_ = bf16[2,2,80,3072]{3,2,1,0:T(8,128)(2,1)S(1)} collective-permute-done((bf16[2,2,80,3072]{3,2,1,0:T(8,128)(2,1)S(1)}, bf16[2,2,80,3072]{3,2,1,0:T(8,128)(2,1)S(1)}, u32[]{:S(2)}, u32[]{:S(2)}) %collective-permute-start.13) | collective-permute-done | bytes 1966112 | tf_op jit(solution)/shard_map/ppermute | solution.py:516
  137.3 3.4 collective-permute-start.32
  140.7 1.6 tile_sums.31
  142.3 4.4 %collective-permute-start.14 = (bf16[2,2,80,3072]{3,2,1,0:T(8,128)(2,1)S(1)}, bf16[2,2,80,3072]{3,2,1,0:T(8,128)(2,1)S(1)}, u32[]{:S(2)}, u32[]{:S(2)}) collective-permute-start(bf16[2,2,80,3072]{3,2,1,0:T(8,128)(2,1)S(1)} %tile_sums.31), channel_id=1, source_target_pairs={{0,8},{2,10},{4,12},{6,14},{8,16},{10,18},{12,20},{14,22},{1,9},{3... | collective-permute-start | bytes 5898248 | tf_op jit(solution)/shard_map/ppermute | solution.py:516
  146.7 1.6 tile_sums.20
  152.1 1.4 collective-permute-start.6
  154.4 22.0 %collective-permute-done.32.refs_3_ = bf16[2,128,3072]{2,1,0:T(8,128)(2,1)S(1)} collective-permute-done((bf16[2,128,3072]{2,1,0:T(8,128)(2,1)S(1)}, bf16[2,128,3072]{2,1,0:T(8,128)(2,1)S(1)}, u32[]{:S(2)}, u32[]{:S(2)}) %collective-permute-start.32) | collective-permute-done | bytes 1572896 | tf_op jit(solution)/shard_map/ppermute | solution.py:516
  177.6 1.5 collective-permute-start.5
  179.1 5.4 %grad_sums.4.refs_3_ = f32[2,2,128,1536]{3,2,1,0:T(8,128)S(1)} custom-call(s32[23]{0:T(128)S(1)} %fusion.12.ids, s32[298]{0:T(512)S(1)} %pad_add_fusion.1.meta_own, s32[298]{0:T(512)S(1)} %collective-permute-done.meta_other, bf16[72,128,128]{2,1,0:T(8,128)(2,1)} %tiles_own.9, bf16[72,128,128]{2,1,0:T(8,128)(2,1)} %collective-permute-done.2.tiles_other, ...), custom_call_target="tpu_custom_call" | custom-call | flops 268435456 | bytes 8388608 | tf_op jit(solution)/shard_map/grad_sums/pallas_call | solution.py:439
  184.5 6.8 %grad_sums.5.refs_4_ = f32[2,2,128,1536]{3,2,1,0:T(8,128)S(1)} custom-call(s32[23]{0:T(128)S(1)} %fusion.12.ids, s32[298]{0:T(512)S(1)} %pad_add_fusion.1.meta_own, s32[298]{0:T(512)S(1)} %collective-permute-done.meta_other, bf16[72,128,128]{2,1,0:T(8,128)(2,1)} %tiles_own.9, bf16[72,128,128]{2,1,0:T(8,128)(2,1)} %collective-permute-done.2.tiles_other, ...), custom_call_target="tpu_custom_call" | custom-call | flops 268435456 | bytes 8388608 | tf_op jit(solution)/shard_map/grad_sums/pallas_call | solution.py:439
  191.3 5.3 %grad_sums.6.refs_4_ = f32[2,2,128,1536]{3,2,1,0:T(8,128)S(1)} custom-call(s32[23]{0:T(128)S(1)} %fusion.12.ids, s32[298]{0:T(512)S(1)} %pad_add_fusion.1.meta_own, s32[298]{0:T(512)S(1)} %collective-permute-done.meta_other, bf16[72,128,128]{2,1,0:T(8,128)(2,1)} %tiles_own.9, bf16[72,128,128]{2,1,0:T(8,128)(2,1)} %collective-permute-done.2.tiles_other, ...), custom_call_target="tpu_custom_call" | custom-call | flops 268435456 | bytes 8388608 | tf_op jit(solution)/shard_map/grad_sums/pallas_call | solution.py:439
  196.7 5.9 %grad_sums.7 = (bf16[2,128,1536]{2,1,0:T(8,128)(2,1)S(1)}, bf16[2,128,1536]{2,1,0:T(8,128)(2,1)}) custom-call(s32[23]{0:T(128)S(1)} %fusion.12.ids, s32[298]{0:T(512)S(1)} %pad_add_fusion.1.meta_own, s32[298]{0:T(512)S(1)} %collective-permute-done.meta_other, bf16[72,128,128]{2,1,0:T(8,128)(2,1)} %tiles_own.9, ...), custom_call_target="tpu_custom_call" | custom-call | flops 268435456 | bytes 8388608 | tf_op jit(solution)/shard_map/grad_sums/pallas_call | solution.py:439
  202.7 1.5 tile_sums.26
  204.1 1.5 collective-permute-start.10
  205.6 1.6 tile_sums.23
  207.3 11.4 %collective-permute-start.7 = (bf16[2,48,3072]{2,1,0:T(8,128)(2,1)}, bf16[2,48,3072]{2,1,0:T(8,128)(2,1)}, u32[]{:S(2)}, u32[]{:S(2)}) collective-permute-start(bf16[2,48,3072]{2,1,0:T(8,128)(2,1)} %tile_sums.23), channel_id=1, source_target_pairs={{0,8},{2,10},{4,12},{6,14},{1,9},{3,11},{5,13},{7,15}} | collective-permute-start | bytes 1769480 | tf_op jit(solution)/shard_map/ppermute | solution.py:516
  218.6 2.0 tile_sums.35
  222.0 2.5 tile_sums.32
  225.3 6.3 %collective-permute-start.15 = (bf16[2,2,80,3072]{3,2,1,0:T(8,128)(2,1)}, bf16[2,2,80,3072]{3,2,1,0:T(8,128)(2,1)}, u32[]{:S(2)}, u32[]{:S(2)}) collective-permute-start(bf16[2,2,80,3072]{3,2,1,0:T(8,128)(2,1)} %tile_sums.32), channel_id=1, source_target_pairs={{0,8},{2,10},{4,12},{6,14},{8,16},{10,18},{12,20},{14,22},{16,24},... | collective-permute-start | bytes 5898248 | tf_op jit(solution)/shard_map/ppermute | solution.py:516
  231.5 2.3 copy-done.2
  234.9 2.1 tile_sums.27
  237.0 1.6 collective-permute-start.11
  238.7 2.5 tile_sums.24
  241.2 2.1 collective-permute-start.8
  243.3 1.3 broadcast_select_fusion.1
  245.9 4.6 %all-to-all-start.1 = ((bf16[2,256,1536]{2,1,0:T(8,128)(2,1)}), bf16[2,256,1536]{2,1,0:T(8,128)(2,1)}, u32[]{:S(2)}, u32[]{:S(2)}) async-start(bf16[2,256,1536]{2,1,0:T(8,128)(2,1)} %pad_maximum_fusion.2), calls=%async_computation.1 | async-start | bytes 3145728 | tf_op jit(solution)/shard_map/all_to_all | solution.py:609
  250.5 2.3 copy-done.3
  256.5 29.6 %collective-permute-done.8.refs_1_ = bf16[2,48,3072]{2,1,0:T(8,128)(2,1)} collective-permute-done((bf16[2,48,3072]{2,1,0:T(8,128)(2,1)}, bf16[2,48,3072]{2,1,0:T(8,128)(2,1)}, u32[]{:S(2)}, u32[]{:S(2)}) %collective-permute-start.8) | collective-permute-done | bytes 589856 | tf_op jit(solution)/shard_map/ppermute | solution.py:516
  286.1 1.5 tile_sums.25
  287.6 4.6 %collective-permute-start.9 = (bf16[2,48,3072]{2,1,0:T(8,128)(2,1)S(1)}, bf16[2,48,3072]{2,1,0:T(8,128)(2,1)S(1)}, u32[]{:S(2)}, u32[]{:S(2)}) collective-permute-start(bf16[2,48,3072]{2,1,0:T(8,128)(2,1)S(1)} %tile_sums.25), channel_id=1, source_target_pairs={{0,8},{2,10},{4,12},{6,14},{8,16},{10,18},{12,20},{14,22},{16,24},... | collective-permute-start | bytes 1769480 | tf_op jit(solution)/shard_map/ppermute | solution.py:516
  292.2 4.4 %collective-permute-done.12.refs_2_ = bf16[2,48,3072]{2,1,0:T(8,128)(2,1)S(1)} collective-permute-done((bf16[2,48,3072]{2,1,0:T(8,128)(2,1)S(1)}, bf16[2,48,3072]{2,1,0:T(8,128)(2,1)S(1)}, u32[]{:S(2)}, u32[]{:S(2)}) %collective-permute-start.12) | collective-permute-done | bytes 589856 | tf_op jit(solution)/shard_map/ppermute | solution.py:516
  296.6 7.9 %collective-permute-done.9.refs_1_ = bf16[2,48,3072]{2,1,0:T(8,128)(2,1)S(1)} collective-permute-done((bf16[2,48,3072]{2,1,0:T(8,128)(2,1)S(1)}, bf16[2,48,3072]{2,1,0:T(8,128)(2,1)S(1)}, u32[]{:S(2)}, u32[]{:S(2)}) %collective-permute-start.9) | collective-permute-done | bytes 589856 | tf_op jit(solution)/shard_map/ppermute | solution.py:516
  304.6 1.8 tile_sums.29
  307.1 3.2 tile_sums.36
  310.2 3.0 fusion.7
  313.3 1.8 convolution_convert_fusion.1
  315.1 4.9 %all-to-all-start.2 = ((bf16[32,16,512]{2,1,0:T(8,128)(2,1)}), bf16[32,16,512]{2,1,0:T(8,128)(2,1)}, u32[]{:S(2)}, u32[]{:S(2)}) async-start(bf16[32,16,512]{2,1,0:T(8,128)(2,1)} %bitcast.37), calls=%async_computation.2 | async-start | bytes 1048576 | tf_op jit(solution)/shard_map/all_to_all | solution.py:620
  320.0 1.7 constant_dynamic-update-slice_fusion.1
  321.7 1.7 constant_dynamic-update-slice_fusion.3
  323.4 16.0 %collective-permute-done.19.refs_2_ = bf16[2,80,3072]{2,1,0:T(8,128)(2,1)} collective-permute-done((bf16[2,80,3072]{2,1,0:T(8,128)(2,1)}, bf16[2,80,3072]{2,1,0:T(8,128)(2,1)}, u32[]{:S(2)}, u32[]{:S(2)}) %collective-permute-start.19) | collective-permute-done | bytes 983072 | tf_op jit(solution)/shard_map/ppermute | solution.py:516
  339.4 2.3 copy-done.4
  341.7 3.5 tile_sums.37
  345.2 2.2 convolution_convert_fusion
  350.2 3.5 all-to-all-start.3
  356.3 12.4 %all-to-all-done.3 = bf16[32,16,512]{2,1,0:T(8,128)(2,1)S(1)} async-done(((bf16[32,16,512]{2,1,0:T(8,128)(2,1)}), bf16[32,16,512]{2,1,0:T(8,128)(2,1)S(1)}, u32[]{:S(2)}, u32[]{:S(2)}) %all-to-all-start.3) | async-done | bytes 524320 | tf_op jit(solution)/shard_map/all_to_all | solution.py:624
  (140 shorter events, 37.2 us)
Async XLA Ops:
  0.6 5.1 %copy-start = (bf16[1536,512]{1,0:T(8,128)(2,1)S(1)}, bf16[1536,512]{1,0:T(8,128)(2,1)}, u32[]{:S(2)}) copy-start(bf16[1536,512]{1,0:T(8,128)(2,1)} %param.10) | copy-start | bytes 4718596
  0.6 3.1 copy-start.33
  0.7 3.0 copy-start.32
  3.2 2.6 copy-start.27
  3.2 10.3 %collective-permute-start.22 = (bf16[128,3072]{1,0:T(8,128)(2,1)S(1)}, bf16[128,3072]{1,0:T(8,128)(2,1)S(1)}, u32[]{:S(2)}, u32[]{:S(2)}) collective-permute-start(bf16[128,3072]{1,0:T(8,128)(2,1)S(1)} %get-tuple-element.18), channel_id=1, source_target_pairs={{0,2},{2,0},{4,6},{6,4},{8,10},{10,8},{12,14},{14,12},{16,18},{18,... | collective-permute-start | bytes 2359304 | tf_op jit(solution)/shard_map/ppermute | solution.py:516
  3.7 60.4 %collective-permute-start.2 = (bf16[72,128,128]{2,1,0:T(8,128)(2,1)}, bf16[72,128,128]{2,1,0:T(8,128)(2,1)}, u32[]{:S(2)}, u32[]{:S(2)}) collective-permute-start(bf16[72,128,128]{2,1,0:T(8,128)(2,1)} %tiles_own.9), channel_id=1, source_target_pairs={{0,2},{2,0},{4,6},{6,4},{8,10},{10,8},{12,14},{14,12},{16,18},{18,... | collective-permute-start | bytes 7077896 | tf_op jit(solution)/shard_map/ppermute | solution.py:516
  8.7 4.8 %copy-start.29 = (s32[72,1]{0,1:T(1,128)S(1)}, s32[72,1]{0,1:T(1,128)}, u32[]{:S(2)}) copy-start(s32[72,1]{0,1:T(1,128)} %param.15) | copy-start | bytes 868
  8.7 25.8 %all-to-all-start = ((bf16[2,256,1536]{2,1,0:T(8,128)(2,1)}), bf16[2,256,1536]{2,1,0:T(8,128)(2,1)}, u32[]{:S(2)}, u32[]{:S(2)}) async-start(bf16[2,256,1536]{2,1,0:T(8,128)(2,1)} %bitcast.7), calls=%async_computation | async-start | bytes 3145728 | tf_op jit(solution)/shard_map/all_to_all | solution.py:554
  13.5 9.9 %copy-start.30 = (s32[72]{0:T(128)S(1)}, s32[72]{0:T(128)}, u32[]{:S(2)}) copy-start(s32[72]{0:T(128)} %param.17) | copy-start | bytes 868
  13.5 9.9 %copy-start.31 = (s32[72]{0:T(128)S(1)}, s32[72]{0:T(128)}, u32[]{:S(2)}) copy-start(s32[72]{0:T(128)} %param.16) | copy-start | bytes 868
  16.0 38.8 %collective-permute-start.23 = (bf16[2,128,3072]{2,1,0:T(8,128)(2,1)S(1)}, bf16[2,128,3072]{2,1,0:T(8,128)(2,1)}, u32[]{:S(2)}, u32[]{:S(2)}) collective-permute-start(bf16[2,128,3072]{2,1,0:T(8,128)(2,1)S(1)} %pad_maximum_fusion.1.refs_0_), channel_id=1, source_target_pairs={{0,8},{2,10},{4,12},{6,14},{8,16},{10,18},{12,20},{14,22},{16,24},... | collective-permute-start | bytes 4718600 | tf_op jit(solution)/shard_map/ppermute | solution.py:516
  22.1 38.0 %collective-permute-start.26 = (bf16[2,128,3072]{2,1,0:T(8,128)(2,1)S(1)}, bf16[2,128,3072]{2,1,0:T(8,128)(2,1)}, u32[]{:S(2)}, u32[]{:S(2)}) collective-permute-start(bf16[2,128,3072]{2,1,0:T(8,128)(2,1)S(1)} %pad_maximum_fusion.1.refs_0_), channel_id=1, source_target_pairs={{8,0},{10,2},{12,4},{14,6},{16,8},{18,10},{20,12},{22,14},{24,16},... | collective-permute-start | bytes 4718600 | tf_op jit(solution)/shard_map/ppermute | solution.py:516
  24.1 12.7 %collective-permute-start = (s32[298]{0:T(512)S(1)}, s32[298]{0:T(512)S(1)}, u32[]{:S(2)}, u32[]{:S(2)}) collective-permute-start(s32[298]{0:T(512)S(1)} %pad_add_fusion.1.meta_own), channel_id=1, source_target_pairs={{0,2},{2,0},{4,6},{6,4},{8,10},{10,8},{12,14},{14,12},{16,18},{18,... | collective-permute-start | bytes 3584 | tf_op jit(solution)/shard_map/ppermute | solution.py:516
  24.1 54.9 %collective-permute-start.35 = (bf16[2,128,3072]{2,1,0:T(8,128)(2,1)S(1)}, bf16[2,128,3072]{2,1,0:T(8,128)(2,1)}, u32[]{:S(2)}, u32[]{:S(2)}) collective-permute-start(bf16[2,128,3072]{2,1,0:T(8,128)(2,1)S(1)} %pad_maximum_fusion.1.refs_0_), channel_id=1, source_target_pairs={{0,4},{2,6},{4,0},{6,2},{8,12},{10,14},{12,8},{14,10},{16,20},{18,... | collective-permute-start | bytes 4718600 | tf_op jit(solution)/shard_map/ppermute | solution.py:516
  36.8 24.6 %collective-permute-start.1 = (bf16[2,128,1536]{2,1,0:T(8,128)(2,1)S(1)}, bf16[2,128,1536]{2,1,0:T(8,128)(2,1)S(1)}, u32[]{:S(2)}, u32[]{:S(2)}) collective-permute-start(bf16[2,128,1536]{2,1,0:T(8,128)(2,1)S(1)} %get-tuple-element.21), channel_id=1, source_target_pairs={{0,2},{2,0},{4,6},{6,4},{8,10},{10,8},{12,14},{14,12},{16,18},{18,... | collective-permute-start | bytes 2359304 | tf_op jit(solution)/shard_map/ppermute | solution.py:516
  54.7 26.2 %collective-permute-start.24 = (bf16[2,128,3072]{2,1,0:T(8,128)(2,1)}, bf16[2,128,3072]{2,1,0:T(8,128)(2,1)}, u32[]{:S(2)}, u32[]{:S(2)}) collective-permute-start(bf16[2,128,3072]{2,1,0:T(8,128)(2,1)} %collective-permute-done.23.refs_1_), channel_id=1, source_target_pairs={{8,16},{10,18},{12,20},{14,22},{16,24},{18,26},{20,28},{22,30},{9,... | collective-permute-start | bytes 4718600 | tf_op jit(solution)/shard_map/ppermute | solution.py:516
  60.1 37.5 %collective-permute-start.27 = (bf16[2,128,3072]{2,1,0:T(8,128)(2,1)}, bf16[2,128,3072]{2,1,0:T(8,128)(2,1)}, u32[]{:S(2)}, u32[]{:S(2)}) collective-permute-start(bf16[2,128,3072]{2,1,0:T(8,128)(2,1)} %collective-permute-done.26.refs_2_), channel_id=1, source_target_pairs={{8,0},{10,2},{12,4},{14,6},{16,8},{18,10},{20,12},{22,14},{9,1},{1... | collective-permute-start | bytes 4718600 | tf_op jit(solution)/shard_map/ppermute | solution.py:516
  62.3 36.0 %collective-permute-start.33 = (bf16[2,128,3072]{2,1,0:T(8,128)(2,1)}, bf16[2,128,3072]{2,1,0:T(8,128)(2,1)}, u32[]{:S(2)}, u32[]{:S(2)}) collective-permute-start(bf16[2,128,3072]{2,1,0:T(8,128)(2,1)} %collective-permute-done.23.refs_1_), channel_id=1, source_target_pairs={{8,12},{10,14},{12,8},{14,10},{16,20},{18,22},{20,16},{22,18},{24,... | collective-permute-start | bytes 4718600 | tf_op jit(solution)/shard_map/ppermute | solution.py:516
  64.1 37.4 %collective-permute-start.34 = (bf16[2,128,3072]{2,1,0:T(8,128)(2,1)}, bf16[2,128,3072]{2,1,0:T(8,128)(2,1)}, u32[]{:S(2)}, u32[]{:S(2)}) collective-permute-start(bf16[2,128,3072]{2,1,0:T(8,128)(2,1)} %collective-permute-done.26.refs_2_), channel_id=1, source_target_pairs={{0,4},{2,6},{4,0},{6,2},{8,12},{10,14},{12,8},{14,10},{16,20},{18,... | collective-permute-start | bytes 4718600 | tf_op jit(solution)/shard_map/ppermute | solution.py:516
  78.3 143.7 %copy-start.1 = (bf16[2,72,128,128]{3,2,1,0:T(8,128)(2,1)}, bf16[2,72,128,128]{3,2,1,0:T(8,128)(2,1)S(1)}, u32[]{:S(2)}) copy-start(bf16[2,72,128,128]{3,2,1,0:T(8,128)(2,1)S(1)} %tile_parts.1.parts) | copy-start | bytes 14155780
  79.1 23.2 %collective-permute-start.16 = (bf16[2,2,80,3072]{3,2,1,0:T(8,128)(2,1)S(1)}, bf16[2,2,80,3072]{3,2,1,0:T(8,128)(2,1)S(1)}, u32[]{:S(2)}, u32[]{:S(2)}) collective-permute-start(bf16[2,2,80,3072]{3,2,1,0:T(8,128)(2,1)S(1)} %tile_sums.33), channel_id=1, source_target_pairs={{24,16},{26,18},{28,20},{30,22},{25,17},{27,19},{29,21},{31,23}} | collective-permute-start | bytes 5898248 | tf_op jit(solution)/shard_map/ppermute | solution.py:516
  80.9 55.5 %collective-permute-start.13 = (bf16[2,2,80,3072]{3,2,1,0:T(8,128)(2,1)S(1)}, bf16[2,2,80,3072]{3,2,1,0:T(8,128)(2,1)S(1)}, u32[]{:S(2)}, u32[]{:S(2)}) collective-permute-start(bf16[2,2,80,3072]{3,2,1,0:T(8,128)(2,1)S(1)} %tile_sums.30), channel_id=1, source_target_pairs={{0,8},{2,10},{4,12},{6,14},{1,9},{3,11},{5,13},{7,15}} | collective-permute-start | bytes 5898248 | tf_op jit(solution)/shard_map/ppermute | solution.py:516
  97.6 8.1 %collective-permute-start.29 = (bf16[2,128,3072]{2,1,0:T(8,128)(2,1)}, bf16[2,128,3072]{2,1,0:T(8,128)(2,1)S(1)}, u32[]{:S(2)}, u32[]{:S(2)}) collective-permute-start(bf16[2,128,3072]{2,1,0:T(8,128)(2,1)} %collective-permute-done.24.refs_1_), channel_id=1, source_target_pairs={{16,24},{18,26},{20,28},{22,30},{17,25},{19,27},{21,29},{23,31}} | collective-permute-start | bytes 4718600 | tf_op jit(solution)/shard_map/ppermute | solution.py:516
  98.3 38.9 %collective-permute-start.31 = (bf16[2,128,3072]{2,1,0:T(8,128)(2,1)}, bf16[2,128,3072]{2,1,0:T(8,128)(2,1)S(1)}, u32[]{:S(2)}, u32[]{:S(2)}) collective-permute-start(bf16[2,128,3072]{2,1,0:T(8,128)(2,1)} %collective-permute-done.27.refs_2_), channel_id=1, source_target_pairs={{8,0},{10,2},{12,4},{14,6},{9,1},{11,3},{13,5},{15,7}} | collective-permute-start | bytes 4718600 | tf_op jit(solution)/shard_map/ppermute | solution.py:516
  101.5 40.8 %collective-permute-start.25 = (bf16[2,128,3072]{2,1,0:T(8,128)(2,1)}, bf16[2,128,3072]{2,1,0:T(8,128)(2,1)S(1)}, u32[]{:S(2)}, u32[]{:S(2)}) collective-permute-start(bf16[2,128,3072]{2,1,0:T(8,128)(2,1)} %collective-permute-done.24.refs_1_), channel_id=1, source_target_pairs={{16,20},{18,22},{20,16},{22,18},{24,28},{26,30},{28,24},{30,26},{1... | collective-permute-start | bytes 4718600 | tf_op jit(solution)/shard_map/ppermute | solution.py:516
  102.2 46.1 %collective-permute-start.28 = (bf16[2,128,3072]{2,1,0:T(8,128)(2,1)}, bf16[2,128,3072]{2,1,0:T(8,128)(2,1)S(1)}, u32[]{:S(2)}, u32[]{:S(2)}) collective-permute-start(bf16[2,128,3072]{2,1,0:T(8,128)(2,1)} %collective-permute-done.27.refs_2_), channel_id=1, source_target_pairs={{0,4},{2,6},{4,0},{6,2},{8,12},{10,14},{12,8},{14,10},{1,5},{3,7},... | collective-permute-start | bytes 4718600 | tf_op jit(solution)/shard_map/ppermute | solution.py:516
  105.7 45.3 %collective-permute-start.30 = (bf16[2,128,3072]{2,1,0:T(8,128)(2,1)S(1)}, bf16[2,128,3072]{2,1,0:T(8,128)(2,1)S(1)}, u32[]{:S(2)}, u32[]{:S(2)}) collective-permute-start(bf16[2,128,3072]{2,1,0:T(8,128)(2,1)S(1)} %collective-permute-done.29.refs_2_), channel_id=1, source_target_pairs={{24,28},{26,30},{28,24},{30,26},{25,29},{27,31},{29,25},{31,27}} | collective-permute-start | bytes 4718600 | tf_op jit(solution)/shard_map/ppermute | solution.py:516
  136.5 70.8 %collective-permute-start.17 = (bf16[2,2,80,3072]{3,2,1,0:T(8,128)(2,1)S(1)}, bf16[2,2,80,3072]{3,2,1,0:T(8,128)(2,1)S(1)}, u32[]{:S(2)}, u32[]{:S(2)}) collective-permute-start(bf16[2,2,80,3072]{3,2,1,0:T(8,128)(2,1)S(1)} %tile_sums.34), channel_id=1, source_target_pairs={{16,8},{18,10},{20,12},{22,14},{24,16},{26,18},{28,20},{30,22},{17... | collective-permute-start | bytes 5898248 | tf_op jit(solution)/shard_map/ppermute | solution.py:516
  137.3 39.2 %collective-permute-start.32 = (bf16[2,128,3072]{2,1,0:T(8,128)(2,1)S(1)}, bf16[2,128,3072]{2,1,0:T(8,128)(2,1)S(1)}, u32[]{:S(2)}, u32[]{:S(2)}) collective-permute-start(bf16[2,128,3072]{2,1,0:T(8,128)(2,1)S(1)} %collective-permute-done.31.refs_3_), channel_id=1, source_target_pairs={{0,4},{2,6},{4,0},{6,2},{1,5},{3,7},{5,1},{7,3}} | collective-permute-start | bytes 4718600 | tf_op jit(solution)/shard_map/ppermute | solution.py:516
  142.3 78.4 %collective-permute-start.14 = (bf16[2,2,80,3072]{3,2,1,0:T(8,128)(2,1)S(1)}, bf16[2,2,80,3072]{3,2,1,0:T(8,128)(2,1)S(1)}, u32[]{:S(2)}, u32[]{:S(2)}) collective-permute-start(bf16[2,2,80,3072]{3,2,1,0:T(8,128)(2,1)S(1)} %tile_sums.31), channel_id=1, source_target_pairs={{0,8},{2,10},{4,12},{6,14},{8,16},{10,18},{12,20},{14,22},{1,9},{3... | collective-permute-start | bytes 5898248 | tf_op jit(solution)/shard_map/ppermute | solution.py:516
  149.5 53.1 %collective-permute-start.4 = (bf16[2,48,3072]{2,1,0:T(8,128)(2,1)}, bf16[2,48,3072]{2,1,0:T(8,128)(2,1)S(1)}, u32[]{:S(2)}, u32[]{:S(2)}) collective-permute-start(bf16[2,48,3072]{2,1,0:T(8,128)(2,1)} %tile_sums.20), channel_id=1, source_target_pairs={{0,4},{2,6},{4,0},{6,2},{8,12},{10,14},{12,8},{14,10},{16,20},{18,... | collective-permute-start | bytes 1769480 | tf_op jit(solution)/shard_map/ppermute | solution.py:516
  152.1 52.1 %collective-permute-start.6 = (bf16[2,48,3072]{2,1,0:T(8,128)(2,1)S(1)}, bf16[2,48,3072]{2,1,0:T(8,128)(2,1)S(1)}, u32[]{:S(2)}, u32[]{:S(2)}) collective-permute-start(bf16[2,48,3072]{2,1,0:T(8,128)(2,1)S(1)} %tile_sums.22), channel_id=1, source_target_pairs={{0,4},{2,6},{4,0},{6,2},{8,12},{10,14},{12,8},{14,10},{16,20},{18,... | collective-permute-start | bytes 1769480 | tf_op jit(solution)/shard_map/ppermute | solution.py:516
  177.6 46.8 %collective-permute-start.5 = (bf16[2,48,3072]{2,1,0:T(8,128)(2,1)S(1)}, bf16[2,48,3072]{2,1,0:T(8,128)(2,1)S(1)}, u32[]{:S(2)}, u32[]{:S(2)}) collective-permute-start(bf16[2,48,3072]{2,1,0:T(8,128)(2,1)S(1)} %tile_sums.21), channel_id=1, source_target_pairs={{0,4},{2,6},{4,0},{6,2},{8,12},{10,14},{12,8},{14,10},{16,20},{18,... | collective-permute-start | bytes 1769480 | tf_op jit(solution)/shard_map/ppermute | solution.py:516
  191.3 5.4 %copy-start.13 = (bf16[2,128,3072]{2,1,0:T(8,128)(2,1)S(1)}, bf16[2,128,3072]{2,1,0:T(8,128)(2,1)}, u32[]{:S(2)}) copy-start(bf16[2,128,3072]{2,1,0:T(8,128)(2,1)} %copy-done.12) | copy-start | bytes 4718596
  191.3 5.4 %copy-start.15 = (bf16[2,128,3072]{2,1,0:T(8,128)(2,1)S(1)}, bf16[2,128,3072]{2,1,0:T(8,128)(2,1)}, u32[]{:S(2)}) copy-start(bf16[2,128,3072]{2,1,0:T(8,128)(2,1)} %copy-done.14) | copy-start | bytes 4718596
  191.3 5.4 %copy-start.17 = (bf16[2,128,3072]{2,1,0:T(8,128)(2,1)S(1)}, bf16[2,128,3072]{2,1,0:T(8,128)(2,1)}, u32[]{:S(2)}) copy-start(bf16[2,128,3072]{2,1,0:T(8,128)(2,1)} %copy-done.16) | copy-start | bytes 4718596
  202.6 1.5 copy-start.20
  202.6 1.5 copy-start.8
  202.6 40.7 %collective-permute-start.36 = (bf16[2,128,1536]{2,1,0:T(8,128)(2,1)}, bf16[2,128,1536]{2,1,0:T(8,128)(2,1)}, u32[]{:S(2)}, u32[]{:S(2)}) collective-permute-start(bf16[2,128,1536]{2,1,0:T(8,128)(2,1)} %get-tuple-element.14), channel_id=1, source_target_pairs={{0,2},{2,0},{4,6},{6,4},{8,10},{10,8},{12,14},{14,12},{16,18},{18,... | collective-permute-start | bytes 2359304 | tf_op jit(solution)/shard_map/ppermute | solution.py:516
  204.1 3.1 copy-start.10
  204.1 27.4 %collective-permute-start.10 = (bf16[2,48,3072]{2,1,0:T(8,128)(2,1)}, bf16[2,48,3072]{2,1,0:T(8,128)(2,1)}, u32[]{:S(2)}, u32[]{:S(2)}) collective-permute-start(bf16[2,48,3072]{2,1,0:T(8,128)(2,1)} %tile_sums.26), channel_id=1, source_target_pairs={{24,16},{26,18},{28,20},{30,22},{25,17},{27,19},{29,21},{31,23}} | collective-permute-start | bytes 1769480 | tf_op jit(solution)/shard_map/ppermute | solution.py:516
  207.3 31.4 %collective-permute-start.7 = (bf16[2,48,3072]{2,1,0:T(8,128)(2,1)}, bf16[2,48,3072]{2,1,0:T(8,128)(2,1)}, u32[]{:S(2)}, u32[]{:S(2)}) collective-permute-start(bf16[2,48,3072]{2,1,0:T(8,128)(2,1)} %tile_sums.23), channel_id=1, source_target_pairs={{0,8},{2,10},{4,12},{6,14},{1,9},{3,11},{5,13},{7,15}} | collective-permute-start | bytes 1769480 | tf_op jit(solution)/shard_map/ppermute | solution.py:516
  220.7 86.4 %collective-permute-start.18 = (bf16[2,2,80,3072]{3,2,1,0:T(8,128)(2,1)}, bf16[2,2,80,3072]{3,2,1,0:T(8,128)(2,1)S(1)}, u32[]{:S(2)}, u32[]{:S(2)}) collective-permute-start(bf16[2,2,80,3072]{3,2,1,0:T(8,128)(2,1)} %tile_sums.35), channel_id=1, source_target_pairs={{8,0},{10,2},{12,4},{14,6},{16,8},{18,10},{20,12},{22,14},{24,16},... | collective-permute-start | bytes 5898248 | tf_op jit(solution)/shard_map/ppermute | solution.py:516
  225.3 81.8 %collective-permute-start.15 = (bf16[2,2,80,3072]{3,2,1,0:T(8,128)(2,1)}, bf16[2,2,80,3072]{3,2,1,0:T(8,128)(2,1)}, u32[]{:S(2)}, u32[]{:S(2)}) collective-permute-start(bf16[2,2,80,3072]{3,2,1,0:T(8,128)(2,1)} %tile_sums.32), channel_id=1, source_target_pairs={{0,8},{2,10},{4,12},{6,14},{8,16},{10,18},{12,20},{14,22},{16,24},... | collective-permute-start | bytes 5898248 | tf_op jit(solution)/shard_map/ppermute | solution.py:516
  231.5 2.3 copy-start.2
  237.0 6.2 %copy-start.21 = (bf16[2,128,1536]{2,1,0:T(8,128)(2,1)S(1)}, bf16[2,128,1536]{2,1,0:T(8,128)(2,1)}, u32[]{:S(2)}) copy-start(bf16[2,128,1536]{2,1,0:T(8,128)(2,1)} %copy-done.20) | copy-start | bytes 2359300
  237.0 16.8 %collective-permute-start.11 = (bf16[2,48,3072]{2,1,0:T(8,128)(2,1)}, bf16[2,48,3072]{2,1,0:T(8,128)(2,1)}, u32[]{:S(2)}, u32[]{:S(2)}) collective-permute-start(bf16[2,48,3072]{2,1,0:T(8,128)(2,1)} %tile_sums.27), channel_id=1, source_target_pairs={{16,8},{18,10},{20,12},{22,14},{24,16},{26,18},{28,20},{30,22},{17... | collective-permute-start | bytes 1769480 | tf_op jit(solution)/shard_map/ppermute | solution.py:516
  241.2 45.0 %collective-permute-start.8 = (bf16[2,48,3072]{2,1,0:T(8,128)(2,1)}, bf16[2,48,3072]{2,1,0:T(8,128)(2,1)}, u32[]{:S(2)}, u32[]{:S(2)}) collective-permute-start(bf16[2,48,3072]{2,1,0:T(8,128)(2,1)} %tile_sums.24), channel_id=1, source_target_pairs={{0,8},{2,10},{4,12},{6,14},{8,16},{10,18},{12,20},{14,22},{1,9},{3... | collective-permute-start | bytes 1769480 | tf_op jit(solution)/shard_map/ppermute | solution.py:516
  245.9 64.4 %all-to-all-start.1 = ((bf16[2,256,1536]{2,1,0:T(8,128)(2,1)}), bf16[2,256,1536]{2,1,0:T(8,128)(2,1)}, u32[]{:S(2)}, u32[]{:S(2)}) async-start(bf16[2,256,1536]{2,1,0:T(8,128)(2,1)} %pad_maximum_fusion.2), calls=%async_computation.1 | async-start | bytes 3145728 | tf_op jit(solution)/shard_map/all_to_all | solution.py:609
  250.5 2.3 copy-start.3
  253.8 32.4 %copy-start.9 = (bf16[2,48,3072]{2,1,0:T(8,128)(2,1)S(1)}, bf16[2,48,3072]{2,1,0:T(8,128)(2,1)}, u32[]{:S(2)}) copy-start(bf16[2,48,3072]{2,1,0:T(8,128)(2,1)} %copy-done.8) | copy-start | bytes 1769476
  253.8 38.4 %collective-permute-start.3 = (bf16[2,48,3072]{2,1,0:T(8,128)(2,1)S(1)}, bf16[2,48,3072]{2,1,0:T(8,128)(2,1)S(1)}, u32[]{:S(2)}, u32[]{:S(2)}) collective-permute-start(bf16[2,48,3072]{2,1,0:T(8,128)(2,1)S(1)} %tile_sums.19), channel_id=1, source_target_pairs={{0,4},{2,6},{4,0},{6,2},{8,12},{10,14},{12,8},{14,10},{16,20},{18,... | collective-permute-start | bytes 1769480 | tf_op jit(solution)/shard_map/ppermute | solution.py:516
  255.2 41.4 %collective-permute-start.12 = (bf16[2,48,3072]{2,1,0:T(8,128)(2,1)S(1)}, bf16[2,48,3072]{2,1,0:T(8,128)(2,1)S(1)}, u32[]{:S(2)}, u32[]{:S(2)}) collective-permute-start(bf16[2,48,3072]{2,1,0:T(8,128)(2,1)S(1)} %tile_sums.28), channel_id=1, source_target_pairs={{8,0},{10,2},{12,4},{14,6},{16,8},{18,10},{20,12},{22,14},{24,16},... | collective-permute-start | bytes 1769480 | tf_op jit(solution)/shard_map/ppermute | solution.py:516
  287.6 16.9 %collective-permute-start.9 = (bf16[2,48,3072]{2,1,0:T(8,128)(2,1)S(1)}, bf16[2,48,3072]{2,1,0:T(8,128)(2,1)S(1)}, u32[]{:S(2)}, u32[]{:S(2)}) collective-permute-start(bf16[2,48,3072]{2,1,0:T(8,128)(2,1)S(1)} %tile_sums.25), channel_id=1, source_target_pairs={{0,8},{2,10},{4,12},{6,14},{8,16},{10,18},{12,20},{14,22},{16,24},... | collective-permute-start | bytes 1769480 | tf_op jit(solution)/shard_map/ppermute | solution.py:516
  307.0 14.7 %collective-permute-start.20 = (bf16[48,3072]{1,0:T(8,128)(2,1)}, bf16[48,3072]{1,0:T(8,128)(2,1)}, u32[]{:S(2)}, u32[]{:S(2)}) collective-permute-start(bf16[48,3072]{1,0:T(8,128)(2,1)} %get-tuple-element.11), channel_id=1, source_target_pairs={{0,2},{2,0},{4,6},{6,4},{8,10},{10,8},{12,14},{14,12},{16,18},{18,... | collective-permute-start | bytes 884744 | tf_op jit(solution)/shard_map/ppermute | solution.py:516
  310.2 29.2 %collective-permute-start.19 = (bf16[2,80,3072]{2,1,0:T(8,128)(2,1)}, bf16[2,80,3072]{2,1,0:T(8,128)(2,1)}, u32[]{:S(2)}, u32[]{:S(2)}) collective-permute-start(bf16[2,80,3072]{2,1,0:T(8,128)(2,1)} %tile_sums.36), channel_id=1, source_target_pairs={{0,4},{2,6},{4,0},{6,2},{8,12},{10,14},{12,8},{14,10},{16,20},{18,... | collective-permute-start | bytes 2949128 | tf_op jit(solution)/shard_map/ppermute | solution.py:516
  313.2 1.8 copy-start.23
  315.1 33.1 %all-to-all-start.2 = ((bf16[32,16,512]{2,1,0:T(8,128)(2,1)}), bf16[32,16,512]{2,1,0:T(8,128)(2,1)}, u32[]{:S(2)}, u32[]{:S(2)}) async-start(bf16[32,16,512]{2,1,0:T(8,128)(2,1)} %bitcast.37), calls=%async_computation.2 | async-start | bytes 1048576 | tf_op jit(solution)/shard_map/all_to_all | solution.py:620
  339.4 2.3 copy-start.4
  341.7 3.5 copy-start.24
  341.7 3.5 copy-start.28
  345.2 8.5 %collective-permute-start.21 = (bf16[80,3072]{1,0:T(8,128)(2,1)}, bf16[80,3072]{1,0:T(8,128)(2,1)S(1)}, u32[]{:S(2)}, u32[]{:S(2)}) collective-permute-start(bf16[80,3072]{1,0:T(8,128)(2,1)} %get-tuple-element.12), channel_id=1, source_target_pairs={{0,2},{2,0},{4,6},{6,4},{8,10},{10,8},{12,14},{14,12},{16,18},{18,... | collective-permute-start | bytes 1474568 | tf_op jit(solution)/shard_map/ppermute | solution.py:516
  347.4 6.3 %copy-start.25 = (bf16[128,3072]{1,0:T(8,128)(2,1)S(1)}, bf16[128,3072]{1,0:T(8,128)(2,1)}, u32[]{:S(2)}) copy-start(bf16[128,3072]{1,0:T(8,128)(2,1)} %constant_dynamic-update-slice_fusion.3) | copy-start | bytes 2359300
  350.2 18.5 %all-to-all-start.3 = ((bf16[32,16,512]{2,1,0:T(8,128)(2,1)}), bf16[32,16,512]{2,1,0:T(8,128)(2,1)S(1)}, u32[]{:S(2)}, u32[]{:S(2)}) async-start(bf16[32,16,512]{2,1,0:T(8,128)(2,1)} %broadcast_in_dim.2), calls=%async_computation.3 | async-start | bytes 1048576 | tf_op jit(solution)/shard_map/all_to_all | solution.py:624
  (11 other events, 11.2 us)
